TPU v7x, 32 devices: a whole 2x2x4 slice. The times are simulated.
32 devices in a mesh: arc: 8 (over y, x, core), par: 4 (over z).
Axes of the slice: x: 2, y: 2, z: 4, core: 2. Of those that a mesh axis runs over, the one named last changes fastest.
Arguments:
- partials: bfloat16 [8, 3, 128, 8192], P('arc', None, 'par'), may hold values from -6 to 6
- epoch_index: int32 [8, 128], P('arc'), may hold values from 0 to 511, as said below
- whitening: float32 [8, 3, 128, 128], P('arc'), may hold values from -2 to 2, as said below
Outputs:
- normal_matrix: float32 [8192, 8192], P('arc', 'par')
Inputs may be any that keep to these rules, and one draw needn't show every extreme that they name: `epoch_index`: in each arc the epoch indices rise strictly; the first is 0 and the last is 511. `whitening`: each block is lower triangular with diagonal entries between 1 and 2.
All inputs are finite; a program needn't handle non-finite values.
Results may differ from a plain program's by a relative error of at most 0.0003.
Values may be sent and summed in bfloat16 or wider, within the bound.
No kernel may reach another device: no remote copies, remote signals or barrier semaphores. Data moves between devices by JAX's collectives and lax.ppermute only.
A program may use at most 128 MiB of HBM per device.

v0:
```python
import math

import jax
import jax.numpy as jnp
from jax import lax
from jax.experimental import pallas as pl
from jax.experimental.pallas import tpu as pltpu
from jax.sharding import PartitionSpec as P


KERNEL_GAIN = 8.0


def mixing_matrices(epoch_index, whitening, epochs, row_scale):
    times_arc = epoch_index.astype(jnp.float32) / jnp.float32(4 * epochs - 1)
    later_time = times_arc[:, :, None]
    earlier_time = times_arc[:, None, :]
    green_part = jnp.minimum(later_time, earlier_time) * (
        1.0 - jnp.maximum(later_time, earlier_time)
    )
    kernel = jnp.eye(epochs, dtype=jnp.float32)[None] + KERNEL_GAIN / epochs * green_part
    mixing = jnp.einsum("acij,ajk->acik", whitening, kernel, precision=lax.Precision.HIGHEST)
    return mixing * row_scale


def gram_matrices(mixing):
    return jnp.einsum("acki,ackj->acij", mixing, mixing, precision=lax.Precision.HIGHEST)


def halves(value):
    high = lax.reduce_precision(value, 8, 7)
    return high.astype(jnp.bfloat16), (value - high).astype(jnp.bfloat16)


def mixed_rows(gram, rows):
    high, low = halves(gram)
    both = jnp.concatenate([high, low], axis=1)
    out = jnp.einsum("aij,ajn->ain", both, rows, preferred_element_type=jnp.float32)
    epochs = gram.shape[1]
    return halves(out[:, :epochs] + out[:, epochs:])


def product(rows, columns):
    contract = (((0, 1), (0, 1)), ((), ()))
    return sum(
        lax.dot_general(part, columns, contract, preferred_element_type=jnp.float32)
        for part in rows
    )


def general_on_device(partials, epoch_index, whitening):
    arc_local = partials.shape[0]
    epochs = epoch_index.shape[1]
    param_count = partials.shape[3]
    arc_count = lax.axis_size("arc")
    par_count = lax.axis_size("par")
    row_block = param_count // arc_count
    col_block = param_count // par_count
    row_scale = 1.0 / math.sqrt(3 * epochs * arc_local * arc_count)
    gram = gram_matrices(mixing_matrices(epoch_index, whitening, epochs, row_scale))
    gram = lax.all_gather(gram, "arc", axis=0, tiled=True)
    rows = lax.all_to_all(partials, "arc", split_axis=3, concat_axis=0, tiled=True)
    rows = lax.all_gather(rows, "par", axis=2, tiled=True)
    columns = lax.all_to_all(partials, "par", split_axis=3, concat_axis=2, tiled=True)
    columns = lax.all_gather(columns, "arc", axis=0, tiled=True)
    mixed = mixed_rows(gram.reshape(-1, epochs, epochs), rows.reshape(-1, epochs, row_block))
    return product(mixed, columns.reshape(-1, epochs, col_block))


def place(z, arrays, choose, blocks, share):
    width = arrays[0].shape[1] // blocks
    depth = sum(arrays[picks[0][1]].shape[0] for picks in choose)
    dtype = arrays[0].dtype

    def body(z_ref, *refs):
        out, part = refs[-2:]
        start = 0
        for picks in choose:
            size = refs[picks[0][1]].shape[0]
            for test, which in picks:

                @pl.when(test(z_ref[0]))
                def _(which=which, start=start, size=size):
                    for i in range(blocks):
                        out[i, start : start + size, :] = refs[which][:, i * width : (i + 1) * width]

            start += size
        for i in range(share):
            part[i] = out[z_ref[0] * share + i]

    vmem = pl.BlockSpec(memory_space=pltpu.VMEM)
    return pl.pallas_call(
        body,
        in_specs=[pl.BlockSpec(memory_space=pltpu.SMEM)] + [vmem] * len(arrays),
        out_specs=[vmem, vmem],
        out_shape=[
            jax.ShapeDtypeStruct((blocks, depth, width), dtype),
            jax.ShapeDtypeStruct((share, depth, width), dtype),
        ],
        cost_estimate=pl.CostEstimate(
            flops=0, bytes_accessed=4 * blocks * depth * width, transcendentals=0
        ),
        name="place",
    )(z.reshape(1), *arrays)


def update(total, slots, gram, component, rows, columns, steps=4):
    arcs, epochs = len(gram), gram[0].shape[-1]
    components = gram[0].shape[0]
    height = rows[0][0].shape[2]
    parts, _, width = columns[0][0][0].shape
    first = total is None
    sizes = [v.shape[1] if at is None else v.shape[1] // components for v, at in rows]
    count = len(rows)
    tile = height // steps
    depth = arcs * epochs

    def body(slot_ref, *refs):
        gram_refs, refs = refs[:arcs], refs[arcs:]
        row_refs, refs = refs[:count], refs[count:]
        col_refs, refs = refs[: count * arcs], refs[count * arcs :]
        out_ref, high_ref, low_ref, col_all = refs[-4:]
        n, m = pl.program_id(0), pl.program_id(1)

        @pl.when((n == 0) & (m == 0))
        def _():
            for slot in range(arcs):
                arc = slot_ref[slot]
                piece = jnp.concatenate([r[arc] for r in row_refs], axis=0)
                matrix = gram_refs[slot][0]
                high = matrix.astype(jnp.bfloat16)
                low = (matrix - high.astype(jnp.float32)).astype(jnp.bfloat16)
                both = jnp.concatenate([high, low], axis=0)
                contract = (((0,), (1,)), ((), ()))
                mixed = lax.dot_general(piece, both, contract, preferred_element_type=jnp.float32)
                mixed = mixed[:, :epochs] + mixed[:, epochs:]
                head = mixed.astype(jnp.bfloat16)
                at = slice(slot * epochs, (slot + 1) * epochs)
                high_ref[:, at] = head
                low_ref[:, at] = (mixed - head.astype(jnp.float32)).astype(jnp.bfloat16)

        @pl.when(m == 0)
        def _():
            for slot in range(arcs):
                start = slot * epochs
                for i, size in enumerate(sizes):
                    col_all[start : start + size, :] = col_refs[i * arcs + slot][0]
                    start += size

        span = pl.ds(pl.multiple_of(m * tile, tile), tile)
        value = jnp.dot(high_ref[span, :], col_all[...], preferred_element_type=jnp.float32)
        value = value + jnp.dot(low_ref[span, :], col_all[...], preferred_element_type=jnp.float32)
        if first:
            out_ref[...] = value
        else:
            out_ref[...] = refs[0][...] + value

    args = list(gram)
    in_specs = [pl.BlockSpec((1, epochs, epochs), lambda n, m, _: (component, 0, 0))] * arcs
    for (v, at), size in zip(rows, sizes):
        block = 0 if at is None else at
        args.append(v)
        in_specs.append(
            pl.BlockSpec((arcs, size, height), lambda n, m, _, block=block: (0, block, 0))
        )
    for (arrays, at), size in zip(columns, sizes):
        block = 0 if at is None else at
        args.extend(arrays)
        in_specs.extend(
            [pl.BlockSpec((1, size, width), lambda n, m, _, block=block: (n, block, 0))] * arcs
        )
    whole = pl.BlockSpec((tile, width), lambda n, m, _: (m, n))
    aliases = {}
    if not first:
        in_specs.append(whole)
        aliases = {len(args) + 1: 0}
        args.append(total)
    return pl.pallas_call(
        body,
        grid_spec=pltpu.PrefetchScalarGridSpec(
            num_scalar_prefetch=1,
            grid=(parts, steps),
            in_specs=in_specs,
            out_specs=whole,
            scratch_shapes=[
                pltpu.VMEM((height, depth), jnp.bfloat16),
                pltpu.VMEM((height, depth), jnp.bfloat16),
                pltpu.VMEM((depth, width), jnp.bfloat16),
            ],
        ),
        out_shape=jax.ShapeDtypeStruct((height, parts * width), jnp.float32),
        input_output_aliases=aliases,
        compiler_params=pltpu.CompilerParams(vmem_limit_bytes=24 * 1024 * 1024),
        cost_estimate=pl.CostEstimate(
            flops=4 * height * parts * width * depth,
            bytes_accessed=8 * height * parts * width,
            transcendentals=0,
        ),
        name="update",
    )(slots, *args)


def on_device(partials, epoch_index, whitening):
    arc_local, components, epoch_block, param_count = partials.shape
    epochs = epoch_index.shape[1]
    arc_count = lax.axis_size("arc")
    par_count = lax.axis_size("par")
    total_arcs = arc_local * arc_count
    row_scale = 1.0 / math.sqrt(3 * epochs * total_arcs)
    z = lax.axis_index("par")
    me = lax.axis_index("arc")
    bottom = z == 0
    top = z == par_count - 1

    first = jnp.where(bottom, 1, z - 1)
    second = jnp.where(bottom, 2, jnp.where(top, z - 2, z + 1))
    third = jnp.where(bottom, 3, jnp.where(top, z - 3, jnp.where(z == 1, 3, 0)))
    order = jnp.stack([z, first, second, third])
    mixing = mixing_matrices(epoch_index, whitening, epochs, row_scale)
    mixing = mixing.reshape(arc_local, components, epochs, par_count, epoch_block)
    mixing = jnp.take(mixing, order, axis=3).reshape(arc_local, components, epochs, epochs)
    gram = gram_matrices(mixing)[0]

    def hop(near, far, v):
        moves = [(i, i ^ (far if i % 2 else near)) for i in range(arc_count)]
        return lax.ppermute(v, "arc", moves)

    even, odd = [0, 2, 4, 6, 1, 5, 3, 7], [0, 4, 2, 6, 1, 3, 5, 7]
    slots = me ^ jnp.where(me % 2 == 1, jnp.array(odd), jnp.array(even))
    slots = slots.astype(jnp.int32)

    def in_plane(v):
        one = hop(2, 4, v)
        two = hop(4, 2, v)
        both = hop(4, 2, one)
        held = [v, one, two, both]
        return held + [hop(1, 1, w) for w in held]

    def exchange(blocks, part):
        rows = lax.all_to_all(blocks, "arc", split_axis=0, concat_axis=0, tiled=True)
        return rows, in_plane(part)

    def along(pairs, v):
        return lax.ppermute(v, "par", pairs)

    pick1 = [(lambda i: i == 0, 1), (lambda i: i > 0, 0)]
    pick2 = [
        (lambda i: i == 0, 3),
        (lambda i: i == 3, 2),
        (lambda i: (i == 1) | (i == 2), 1),
    ]
    pick3 = [
        (lambda i: i == 0, 5),
        (lambda i: i == 1, 3),
        (lambda i: i == 2, 2),
        (lambda i: i == 3, 4),
    ]
    share = arc_count // par_count

    own = partials.reshape(components * epoch_block, param_count)
    blocks, part = place(z, [own], [[(lambda i: i >= 0, 0)]], arc_count, share)
    own_rows, own_columns = exchange(blocks, part)
    grams = in_plane(gram)
    total = None
    for c in range(components):
        up = [own[c * epoch_block : (c + 1) * epoch_block]]
        down = list(up)
        for step in range(par_count - 1):
            pairs = [(i, i + 1) for i in range(step, par_count - 1)]
            up.append(along(pairs, up[-1]))
            pairs = [(par_count - 1 - i, par_count - 1 - j) for i, j in pairs]
            down.append(along(pairs, down[-1]))
        arrived = [v for both in zip(up[1:], down[1:]) for v in both]
        blocks, part = place(z, arrived, [pick1, pick2, pick3], arc_count, share)
        rows, columns = exchange(blocks, part)
        total = update(
            total, slots, grams, c, [(own_rows, c), (rows, None)],
            [(own_columns, c), (columns, None)],
        )
    return total


def solution(mesh):
    placed = (P("arc", None, "par", None), P("arc", None), P("arc", None, None, None))
    special = mesh.shape["par"] == 4 and mesh.shape["arc"] == 8

    def body(*args):
        return on_device(*args)

    return jax.shard_map(
        body if special else general_on_device,
        mesh=mesh,
        in_specs=placed,
        out_specs=P("arc", "par"),
        check_vma=False,
    )
```

profile of v0, /device:TPU:0, one launch (start us, length us, event | category | flops | bytes accessed | tf_op | source)
XLA Modules:
  0.0 256.4 jit_solution(4695199911863295392)
XLA Ops:
  0.0 2.6 %slice_bitcast_fusion = (bf16[32,8192]{1,0:T(8,128)(2,1)}, bf16[32,8192]{1,0:T(8,128)(2,1)}, bf16[32,8192]{1,0:T(8,128)(2,1)}) fusion(bf16[1,3,32,8192]{3,2,1,0:T(8,128)(2,1)} %param.5), kind=kLoop, calls=%fused_computation.2 | loop fusion | bytes 3145728 | tf_op jit(solution)/shard_map/slice | solution.py:266
  2.6 5.0 %collective-permute-start.40 = (bf16[32,8192]{1,0:T(8,128)(2,1)}, bf16[32,8192]{1,0:T(8,128)(2,1)S(1)}, u32[]{:S(2)}, u32[]{:S(2)}) collective-permute-start(bf16[32,8192]{1,0:T(8,128)(2,1)} %get-tuple-element.21), channel_id=1, source_target_pairs={{0,1},{1,2},{2,3},{4,5},{5,6},{6,7},{8,9},{9,10},{10,11},{12,13},{... | collective-permute-start | bytes 1572872 | tf_op jit(solution)/shard_map/ppermute | solution.py:244
  7.6 1.3 collective-permute-start.41
  8.9 2.8 %place.4 = (bf16[8,96,1024]{2,1,0:T(8,128)(2,1)}, bf16[2,96,1024]{2,1,0:T(8,128)(2,1)}) custom-call(s32[1]{0:T(128)} %bitcast.z_ref, bf16[96,8192]{1,0:T(8,128)(2,1)} %bitcast.35), custom_call_target="tpu_custom_call" | custom-call | bytes 3145728 | tf_op jit(solution)/shard_map/place/pallas_call | solution.py:92
  11.7 3.9 %all-to-all-start = ((bf16[8,96,1024]{2,1,0:T(8,128)(2,1)}), bf16[8,96,1024]{2,1,0:T(8,128)(2,1)S(1)}, u32[]{:S(2)}, u32[]{:S(2)}) async-start(bf16[8,96,1024]{2,1,0:T(8,128)(2,1)} %get-tuple-element.13), calls=%async_computation | async-start | bytes 3145728 | tf_op jit(solution)/shard_map/all_to_all | solution.py:240
  15.6 3.5 %collective-permute-done.40.refs_0_ = bf16[32,8192]{1,0:T(8,128)(2,1)S(1)} collective-permute-done((bf16[32,8192]{1,0:T(8,128)(2,1)}, bf16[32,8192]{1,0:T(8,128)(2,1)S(1)}, u32[]{:S(2)}, u32[]{:S(2)}) %collective-permute-start.40) | collective-permute-done | bytes 524320 | tf_op jit(solution)/shard_map/ppermute | solution.py:244
  19.0 1.5 collective-permute-start.42
  20.6 2.5 collective-permute-done.41.refs_1_
  23.1 1.3 collective-permute-start.43
  25.6 1.5 collective-permute-start.44
  27.2 11.4 %collective-permute-done.43.refs_3_ = bf16[32,8192]{1,0:T(8,128)(2,1)} collective-permute-done((bf16[32,8192]{1,0:T(8,128)(2,1)S(1)}, bf16[32,8192]{1,0:T(8,128)(2,1)}, u32[]{:S(2)}, u32[]{:S(2)}) %collective-permute-start.43) | collective-permute-done | bytes 524320 | tf_op jit(solution)/shard_map/ppermute | solution.py:244
  38.6 1.3 collective-permute-start.45
  40.4 1.6 collective-permute-start
  42.0 6.2 %collective-permute-start.27 = (bf16[32,8192]{1,0:T(8,128)(2,1)}, bf16[32,8192]{1,0:T(8,128)(2,1)}, u32[]{:S(2)}, u32[]{:S(2)}) collective-permute-start(bf16[32,8192]{1,0:T(8,128)(2,1)} %get-tuple-element.23), channel_id=1, source_target_pairs={{0,1},{1,2},{2,3},{4,5},{5,6},{6,7},{8,9},{9,10},{10,11},{12,13},{... | collective-permute-start | bytes 1572872 | tf_op jit(solution)/shard_map/ppermute | solution.py:244
  48.1 1.3 collective-permute-start.28
  49.4 1.6 collective-permute-start.1
  51.0 4.2 %collective-permute-done.45.refs_5_ = bf16[32,8192]{1,0:T(8,128)(2,1)} collective-permute-done((bf16[32,8192]{1,0:T(8,128)(2,1)}, bf16[32,8192]{1,0:T(8,128)(2,1)}, u32[]{:S(2)}, u32[]{:S(2)}) %collective-permute-start.45) | collective-permute-done | bytes 524320 | tf_op jit(solution)/shard_map/ppermute | solution.py:244
  55.2 1.9 collective-permute-start.2
  57.1 3.3 %place.7 = (bf16[8,96,1024]{2,1,0:T(8,128)(2,1)}, bf16[2,96,1024]{2,1,0:T(8,128)(2,1)}) custom-call(s32[1]{0:T(128)} %bitcast.z_ref, bf16[32,8192]{1,0:T(8,128)(2,1)} %copy-done.35, bf16[32,8192]{1,0:T(8,128)(2,1)} %copy-done.36, bf16[32,8192]{1,0:T(8,128)(2,1)} %collective-permute-done.42.refs_2_, bf16[32,8192]{1,0:T(8,128)(2,1)} %collective-permute-done.43.refs_3_, ...), custom_call_target="tpu_custom_call" | custom-call | bytes 3145728 | tf_op jit(solution)/shard_map/place/pallas_call | solution.py:92
  61.1 3.6 %all-to-all-start.3 = ((bf16[8,96,1024]{2,1,0:T(8,128)(2,1)}), bf16[8,96,1024]{2,1,0:T(8,128)(2,1)S(1)}, u32[]{:S(2)}, u32[]{:S(2)}) async-start(bf16[8,96,1024]{2,1,0:T(8,128)(2,1)} %get-tuple-element.19), calls=%async_computation.3 | async-start | bytes 3145728 | tf_op jit(solution)/shard_map/all_to_all | solution.py:240
  64.7 1.9 collective-permute-start.13
  67.3 1.3 collective-permute-start.30
  68.6 1.6 collective-permute-start.14
  70.2 1.6 collective-permute-done.5.refs_6_
  72.5 5.3 %collective-permute-start.7 = (bf16[32,8192]{1,0:T(8,128)(2,1)}, bf16[32,8192]{1,0:T(8,128)(2,1)}, u32[]{:S(2)}, u32[]{:S(2)}) collective-permute-start(bf16[32,8192]{1,0:T(8,128)(2,1)} %get-tuple-element.22), channel_id=1, source_target_pairs={{0,1},{1,2},{2,3},{4,5},{5,6},{6,7},{8,9},{9,10},{10,11},{12,13},{... | collective-permute-start | bytes 1572872 | tf_op jit(solution)/shard_map/ppermute | solution.py:244
  77.8 15.4 %collective-permute-done.13.refs_11_ = bf16[2,96,1024]{2,1,0:T(8,128)(2,1)} collective-permute-done((bf16[2,96,1024]{2,1,0:T(8,128)(2,1)}, bf16[2,96,1024]{2,1,0:T(8,128)(2,1)}, u32[]{:S(2)}, u32[]{:S(2)}) %collective-permute-start.13) | collective-permute-done | bytes 393248 | tf_op jit(solution)/shard_map/ppermute | solution.py:226
  93.2 1.3 collective-permute-start.8
  95.4 1.3 collective-permute-start.32
  96.7 1.5 collective-permute-start.9
  98.1 12.1 %collective-permute-done.8.refs_1_ = bf16[32,8192]{1,0:T(8,128)(2,1)} collective-permute-done((bf16[32,8192]{1,0:T(8,128)(2,1)}, bf16[32,8192]{1,0:T(8,128)(2,1)}, u32[]{:S(2)}, u32[]{:S(2)}) %collective-permute-start.8) | collective-permute-done | bytes 524320 | tf_op jit(solution)/shard_map/ppermute | solution.py:244
  110.2 1.3 collective-permute-start.10
  112.3 1.6 collective-permute-done.6.refs_7_
  114.6 1.5 collective-permute-start.15
  116.2 5.2 %collective-permute-done.32.refs_5_ = bf16[32,8192]{1,0:T(8,128)(2,1)S(1)} collective-permute-done((bf16[32,8192]{1,0:T(8,128)(2,1)S(1)}, bf16[32,8192]{1,0:T(8,128)(2,1)S(1)}, u32[]{:S(2)}, u32[]{:S(2)}) %collective-permute-start.32) | collective-permute-done | bytes 524320 | tf_op jit(solution)/shard_map/ppermute | solution.py:244
  122.2 3.3 %place.6 = (bf16[8,96,1024]{2,1,0:T(8,128)(2,1)}, bf16[2,96,1024]{2,1,0:T(8,128)(2,1)}) custom-call(s32[1]{0:T(128)} %bitcast.z_ref, bf16[32,8192]{1,0:T(8,128)(2,1)} %collective-permute-done.27.refs_0_, bf16[32,8192]{1,0:T(8,128)(2,1)} %collective-permute-done.28.refs_1_, bf16[32,8192]{1,0:T(8,128)(2,1)} %copy-done.37, bf16[32,8192]{1,0:T(8,128)(2,1)} %copy-done.38, ...), custom_call_target="tpu_custom_call" | custom-call | bytes 3145728 | tf_op jit(solution)/shard_map/place/pallas_call | solution.py:92
  125.4 4.3 %all-to-all-start.2 = ((bf16[8,96,1024]{2,1,0:T(8,128)(2,1)}), bf16[8,96,1024]{2,1,0:T(8,128)(2,1)}, u32[]{:S(2)}, u32[]{:S(2)}) async-start(bf16[8,96,1024]{2,1,0:T(8,128)(2,1)} %get-tuple-element.17), calls=%async_computation.2 | async-start | bytes 3145728 | tf_op jit(solution)/shard_map/all_to_all | solution.py:240
  129.8 1.5 collective-permute-start.11
  131.2 1.3 collective-permute-start.12
  133.0 1.6 collective-permute-start.46
  134.6 1.5 collective-permute-start.47
  137.5 10.2 %collective-permute-done.12.refs_5_ = bf16[32,8192]{1,0:T(8,128)(2,1)} collective-permute-done((bf16[32,8192]{1,0:T(8,128)(2,1)}, bf16[32,8192]{1,0:T(8,128)(2,1)}, u32[]{:S(2)}, u32[]{:S(2)}) %collective-permute-start.12) | collective-permute-done | bytes 524320 | tf_op jit(solution)/shard_map/ppermute | solution.py:244
  147.7 1.6 collective-permute-start.34
  149.3 9.6 %collective-permute-done.46.refs_19_ = bf16[2,96,1024]{2,1,0:T(8,128)(2,1)} collective-permute-done((bf16[2,96,1024]{2,1,0:T(8,128)(2,1)}, bf16[2,96,1024]{2,1,0:T(8,128)(2,1)}, u32[]{:S(2)}, u32[]{:S(2)}) %collective-permute-start.46) | collective-permute-done | bytes 393248 | tf_op jit(solution)/shard_map/ppermute | solution.py:226
  158.9 1.5 collective-permute-start.48
  160.4 3.3 %place.5 = (bf16[8,96,1024]{2,1,0:T(8,128)(2,1)}, bf16[2,96,1024]{2,1,0:T(8,128)(2,1)}) custom-call(s32[1]{0:T(128)} %bitcast.z_ref, bf16[32,8192]{1,0:T(8,128)(2,1)} %collective-permute-done.7.refs_0_, bf16[32,8192]{1,0:T(8,128)(2,1)} %collective-permute-done.8.refs_1_, bf16[32,8192]{1,0:T(8,128)(2,1)} %collective-permute-done.9.refs_2_, ...), custom_call_target="tpu_custom_call" | custom-call | bytes 3145728 | tf_op jit(solution)/shard_map/place/pallas_call | solution.py:92
  164.2 3.1 %collective-permute-done.33.refs_19_ = bf16[2,96,1024]{2,1,0:T(8,128)(2,1)} collective-permute-done((bf16[2,96,1024]{2,1,0:T(8,128)(2,1)}, bf16[2,96,1024]{2,1,0:T(8,128)(2,1)}, u32[]{:S(2)}, u32[]{:S(2)}) %collective-permute-start.33) | collective-permute-done | bytes 393248 | tf_op jit(solution)/shard_map/ppermute | solution.py:226
  167.8 1.5 collective-permute-start.35
  169.3 5.8 %collective-permute-done.48.refs_21_ = bf16[2,96,1024]{2,1,0:T(8,128)(2,1)} collective-permute-done((bf16[2,96,1024]{2,1,0:T(8,128)(2,1)}, bf16[2,96,1024]{2,1,0:T(8,128)(2,1)}, u32[]{:S(2)}, u32[]{:S(2)}) %collective-permute-start.48) | collective-permute-done | bytes 393248 | tf_op jit(solution)/shard_map/ppermute | solution.py:226
  176.0 1.2 collective-permute-start.21
  177.2 4.5 %all-to-all-start.1 = ((bf16[8,96,1024]{2,1,0:T(8,128)(2,1)}), bf16[8,96,1024]{2,1,0:T(8,128)(2,1)}, u32[]{:S(2)}, u32[]{:S(2)}) async-start(bf16[8,96,1024]{2,1,0:T(8,128)(2,1)} %get-tuple-element.14), calls=%async_computation.1 | async-start | bytes 3145728 | tf_op jit(solution)/shard_map/all_to_all | solution.py:240
  182.3 1.7 collective-permute-start.22
  185.0 1.0 copy-done.3
  186.0 1.0 copy-done.5
  186.9 1.0 copy-done.9
  190.7 15.7 %update.3.refs_26_ = f32[1024,2048]{1,0:T(8,128)} custom-call(s32[8]{0:T(128)S(1)} %fusion.13.slot_ref, f32[3,128,128]{2,1,0:T(8,128)S(1)} %fusion.17.refs_0_, f32[3,128,128]{2,1,0:T(8,128)} %collective-permute-done.refs_1_, f32[3,128,128]{2,1,0:T(8,128)S(1)} %copy-done.26, f32[3,128,128]{2,1,0:T(8,128)} %collective-permute-done.2.refs_3_, ...), custom_call_target="tpu_custom_call" | custom-call | flops 8589934592 | bytes 16777216 | tf_op jit(solution)/shard_map/update/pallas_call | solution.py:178
  207.7 17.1 %update.4.refs_26_ = f32[1024,2048]{1,0:T(8,128)} custom-call(s32[8]{0:T(128)S(1)} %fusion.13.slot_ref, f32[3,128,128]{2,1,0:T(8,128)S(1)} %fusion.17.refs_0_, f32[3,128,128]{2,1,0:T(8,128)} %collective-permute-done.refs_1_, f32[3,128,128]{2,1,0:T(8,128)S(1)} %copy-done.27, ...), custom_call_target="tpu_custom_call", output_to_operand_aliasing={{}: (27, {})} | custom-call | flops 8589934592 | bytes 16777216 | tf_op jit(solution)/shard_map/update/pallas_call | solution.py:178
  227.9 1.0 copy-done.2
  228.9 1.0 copy-done.7
  229.9 1.0 copy-done.11
  230.9 1.0 copy-done.14
  231.9 1.0 copy-done.16
  232.8 1.0 copy-done.18
  234.8 1.0 copy-done.22
  239.6 16.8 %update.5 = f32[1024,2048]{1,0:T(8,128)} custom-call(s32[8]{0:T(128)S(1)} %fusion.13.slot_ref, f32[3,128,128]{2,1,0:T(8,128)S(1)} %fusion.17.refs_0_, f32[3,128,128]{2,1,0:T(8,128)} %collective-permute-done.refs_1_, f32[3,128,128]{2,1,0:T(8,128)S(1)} %copy-done.28, f32[3,128,128]{2,1,0:T(8,128)} %collective-permute-done.2.refs_3_, ...), custom_call_target="tpu_custom_call", output_to_operand_aliasing={{}: (27, {})} | custom-call | flops 8589934592 | bytes 16777216 | tf_op jit(solution)/shard_map/update/pallas_call | solution.py:178
  (158 shorter events, 24.4 us)
Async XLA Ops:
  0.0 24.6 %copy-start = (f32[1,3,128,128]{3,2,1,0:T(8,128)S(1)}, f32[1,3,128,128]{3,2,1,0:T(8,128)}, u32[]{:S(2)}) copy-start(f32[1,3,128,128]{3,2,1,0:T(8,128)} %param.7) | copy-start | bytes 589828
  2.6 16.4 %collective-permute-start.40 = (bf16[32,8192]{1,0:T(8,128)(2,1)}, bf16[32,8192]{1,0:T(8,128)(2,1)S(1)}, u32[]{:S(2)}, u32[]{:S(2)}) collective-permute-start(bf16[32,8192]{1,0:T(8,128)(2,1)} %get-tuple-element.21), channel_id=1, source_target_pairs={{0,1},{1,2},{2,3},{4,5},{5,6},{6,7},{8,9},{9,10},{10,11},{12,13},{... | collective-permute-start | bytes 1572872 | tf_op jit(solution)/shard_map/ppermute | solution.py:244
  7.6 15.5 %collective-permute-start.41 = (bf16[32,8192]{1,0:T(8,128)(2,1)}, bf16[32,8192]{1,0:T(8,128)(2,1)S(1)}, u32[]{:S(2)}, u32[]{:S(2)}) collective-permute-start(bf16[32,8192]{1,0:T(8,128)(2,1)} %get-tuple-element.21), channel_id=1, source_target_pairs={{3,2},{2,1},{1,0},{7,6},{6,5},{5,4},{11,10},{10,9},{9,8},{15,14},{... | collective-permute-start | bytes 1572872 | tf_op jit(solution)/shard_map/ppermute | solution.py:244
  11.7 48.8 %all-to-all-start = ((bf16[8,96,1024]{2,1,0:T(8,128)(2,1)}), bf16[8,96,1024]{2,1,0:T(8,128)(2,1)S(1)}, u32[]{:S(2)}, u32[]{:S(2)}) async-start(bf16[8,96,1024]{2,1,0:T(8,128)(2,1)} %get-tuple-element.13), calls=%async_computation | async-start | bytes 3145728 | tf_op jit(solution)/shard_map/all_to_all | solution.py:240
  19.0 21.4 %copy-start.35 = (bf16[32,8192]{1,0:T(8,128)(2,1)}, bf16[32,8192]{1,0:T(8,128)(2,1)S(1)}, u32[]{:S(2)}) copy-start(bf16[32,8192]{1,0:T(8,128)(2,1)S(1)} %collective-permute-done.40.refs_0_) | copy-start | bytes 1572868
  19.0 6.6 %collective-permute-start.42 = (bf16[32,8192]{1,0:T(8,128)(2,1)S(1)}, bf16[32,8192]{1,0:T(8,128)(2,1)}, u32[]{:S(2)}, u32[]{:S(2)}) collective-permute-start(bf16[32,8192]{1,0:T(8,128)(2,1)S(1)} %collective-permute-done.40.refs_0_), channel_id=1, source_target_pairs={{1,2},{2,3},{5,6},{6,7},{9,10},{10,11},{13,14},{14,15},{17,18},{18... | collective-permute-start | bytes 1572872 | tf_op jit(solution)/shard_map/ppermute | solution.py:244
  23.1 17.3 %copy-start.36 = (bf16[32,8192]{1,0:T(8,128)(2,1)}, bf16[32,8192]{1,0:T(8,128)(2,1)S(1)}, u32[]{:S(2)}) copy-start(bf16[32,8192]{1,0:T(8,128)(2,1)S(1)} %collective-permute-done.41.refs_1_) | copy-start | bytes 1572868
  23.1 15.5 %collective-permute-start.43 = (bf16[32,8192]{1,0:T(8,128)(2,1)S(1)}, bf16[32,8192]{1,0:T(8,128)(2,1)}, u32[]{:S(2)}, u32[]{:S(2)}) collective-permute-start(bf16[32,8192]{1,0:T(8,128)(2,1)S(1)} %collective-permute-done.41.refs_1_), channel_id=1, source_target_pairs={{2,1},{1,0},{6,5},{5,4},{10,9},{9,8},{14,13},{13,12},{18,17},{17,1... | collective-permute-start | bytes 1572872 | tf_op jit(solution)/shard_map/ppermute | solution.py:244
  25.6 25.4 %collective-permute-start.44 = (bf16[32,8192]{1,0:T(8,128)(2,1)}, bf16[32,8192]{1,0:T(8,128)(2,1)}, u32[]{:S(2)}, u32[]{:S(2)}) collective-permute-start(bf16[32,8192]{1,0:T(8,128)(2,1)} %collective-permute-done.42.refs_2_), channel_id=1, source_target_pairs={{2,3},{6,7},{10,11},{14,15},{18,19},{22,23},{26,27},{30,31}} | collective-permute-start | bytes 1572872 | tf_op jit(solution)/shard_map/ppermute | solution.py:244
  38.6 16.6 %collective-permute-start.45 = (bf16[32,8192]{1,0:T(8,128)(2,1)}, bf16[32,8192]{1,0:T(8,128)(2,1)}, u32[]{:S(2)}, u32[]{:S(2)}) collective-permute-start(bf16[32,8192]{1,0:T(8,128)(2,1)} %collective-permute-done.43.refs_3_), channel_id=1, source_target_pairs={{1,0},{5,4},{9,8},{13,12},{17,16},{21,20},{25,24},{29,28}} | collective-permute-start | bytes 1572872 | tf_op jit(solution)/shard_map/ppermute | solution.py:244
  40.4 9.0 %collective-permute-start = (f32[3,128,128]{2,1,0:T(8,128)S(1)}, f32[3,128,128]{2,1,0:T(8,128)}, u32[]{:S(2)}, u32[]{:S(2)}) collective-permute-start(f32[3,128,128]{2,1,0:T(8,128)S(1)} %fusion.17.refs_0_), channel_id=1, source_target_pairs={{0,8},{4,20},{8,0},{12,28},{16,24},{20,4},{24,16},{28,12},{1,9},{5... | collective-permute-start | bytes 589832 | tf_op jit(solution)/shard_map/ppermute | solution.py:226
  42.0 24.6 %collective-permute-start.27 = (bf16[32,8192]{1,0:T(8,128)(2,1)}, bf16[32,8192]{1,0:T(8,128)(2,1)}, u32[]{:S(2)}, u32[]{:S(2)}) collective-permute-start(bf16[32,8192]{1,0:T(8,128)(2,1)} %get-tuple-element.23), channel_id=1, source_target_pairs={{0,1},{1,2},{2,3},{4,5},{5,6},{6,7},{8,9},{9,10},{10,11},{12,13},{... | collective-permute-start | bytes 1572872 | tf_op jit(solution)/shard_map/ppermute | solution.py:244
  48.1 19.2 %collective-permute-start.28 = (bf16[32,8192]{1,0:T(8,128)(2,1)}, bf16[32,8192]{1,0:T(8,128)(2,1)}, u32[]{:S(2)}, u32[]{:S(2)}) collective-permute-start(bf16[32,8192]{1,0:T(8,128)(2,1)} %get-tuple-element.23), channel_id=1, source_target_pairs={{3,2},{2,1},{1,0},{7,6},{6,5},{5,4},{11,10},{10,9},{9,8},{15,14},{... | collective-permute-start | bytes 1572872 | tf_op jit(solution)/shard_map/ppermute | solution.py:244
  49.4 11.0 %collective-permute-start.1 = (f32[3,128,128]{2,1,0:T(8,128)S(1)}, f32[3,128,128]{2,1,0:T(8,128)S(1)}, u32[]{:S(2)}, u32[]{:S(2)}) collective-permute-start(f32[3,128,128]{2,1,0:T(8,128)S(1)} %fusion.17.refs_0_), channel_id=1, source_target_pairs={{0,16},{4,12},{8,24},{12,4},{16,0},{20,28},{24,8},{28,20},{1,17},{... | collective-permute-start | bytes 589832 | tf_op jit(solution)/shard_map/ppermute | solution.py:226
  51.0 13.6 %collective-permute-start.3 = (f32[3,128,128]{2,1,0:T(8,128)S(1)}, f32[3,128,128]{2,1,0:T(8,128)}, u32[]{:S(2)}, u32[]{:S(2)}) collective-permute-start(f32[3,128,128]{2,1,0:T(8,128)S(1)} %fusion.17.refs_0_), channel_id=1, source_target_pairs={{0,4},{4,0},{8,12},{12,8},{16,20},{20,16},{24,28},{28,24},{1,5},{5... | collective-permute-start | bytes 589832 | tf_op jit(solution)/shard_map/ppermute | solution.py:226
  55.2 13.4 %collective-permute-start.2 = (f32[3,128,128]{2,1,0:T(8,128)}, f32[3,128,128]{2,1,0:T(8,128)}, u32[]{:S(2)}, u32[]{:S(2)}) collective-permute-start(f32[3,128,128]{2,1,0:T(8,128)} %collective-permute-done.refs_1_), channel_id=1, source_target_pairs={{0,16},{4,12},{8,24},{12,4},{16,0},{20,28},{24,8},{28,20},{1,17},{... | collective-permute-start | bytes 589832 | tf_op jit(solution)/shard_map/ppermute | solution.py:226
  60.4 9.8 %collective-permute-start.4 = (f32[3,128,128]{2,1,0:T(8,128)}, f32[3,128,128]{2,1,0:T(8,128)}, u32[]{:S(2)}, u32[]{:S(2)}) collective-permute-start(f32[3,128,128]{2,1,0:T(8,128)} %collective-permute-done.refs_1_), channel_id=1, source_target_pairs={{0,4},{4,0},{8,12},{12,8},{16,20},{20,16},{24,28},{28,24},{1,5},{5... | collective-permute-start | bytes 589832 | tf_op jit(solution)/shard_map/ppermute | solution.py:226
  61.1 64.4 %all-to-all-start.3 = ((bf16[8,96,1024]{2,1,0:T(8,128)(2,1)}), bf16[8,96,1024]{2,1,0:T(8,128)(2,1)S(1)}, u32[]{:S(2)}, u32[]{:S(2)}) async-start(bf16[8,96,1024]{2,1,0:T(8,128)(2,1)} %get-tuple-element.19), calls=%async_computation.3 | async-start | bytes 3145728 | tf_op jit(solution)/shard_map/all_to_all | solution.py:240
  64.7 28.6 %collective-permute-start.13 = (bf16[2,96,1024]{2,1,0:T(8,128)(2,1)}, bf16[2,96,1024]{2,1,0:T(8,128)(2,1)}, u32[]{:S(2)}, u32[]{:S(2)}) collective-permute-start(bf16[2,96,1024]{2,1,0:T(8,128)(2,1)} %get-tuple-element.15.refs_10_), channel_id=1, source_target_pairs={{0,8},{4,20},{8,0},{12,28},{16,24},{20,4},{24,16},{28,12},{1,9},{5... | collective-permute-start | bytes 1179656 | tf_op jit(solution)/shard_map/ppermute | solution.py:226
  66.6 28.0 %collective-permute-start.29 = (bf16[32,8192]{1,0:T(8,128)(2,1)}, bf16[32,8192]{1,0:T(8,128)(2,1)S(1)}, u32[]{:S(2)}, u32[]{:S(2)}) collective-permute-start(bf16[32,8192]{1,0:T(8,128)(2,1)} %collective-permute-done.27.refs_0_), channel_id=1, source_target_pairs={{1,2},{2,3},{5,6},{6,7},{9,10},{10,11},{13,14},{14,15},{17,18},{18... | collective-permute-start | bytes 1572872 | tf_op jit(solution)/shard_map/ppermute | solution.py:244
  67.3 28.0 %collective-permute-start.30 = (bf16[32,8192]{1,0:T(8,128)(2,1)}, bf16[32,8192]{1,0:T(8,128)(2,1)S(1)}, u32[]{:S(2)}, u32[]{:S(2)}) collective-permute-start(bf16[32,8192]{1,0:T(8,128)(2,1)} %collective-permute-done.28.refs_1_), channel_id=1, source_target_pairs={{2,1},{1,0},{6,5},{5,4},{10,9},{9,8},{14,13},{13,12},{18,17},{17,1... | collective-permute-start | bytes 1572872 | tf_op jit(solution)/shard_map/ppermute | solution.py:244
  68.6 25.9 %collective-permute-start.14 = (bf16[2,96,1024]{2,1,0:T(8,128)(2,1)}, bf16[2,96,1024]{2,1,0:T(8,128)(2,1)}, u32[]{:S(2)}, u32[]{:S(2)}) collective-permute-start(bf16[2,96,1024]{2,1,0:T(8,128)(2,1)} %get-tuple-element.15.refs_10_), channel_id=1, source_target_pairs={{0,16},{4,12},{8,24},{12,4},{16,0},{20,28},{24,8},{28,20},{1,17},{... | collective-permute-start | bytes 1179656 | tf_op jit(solution)/shard_map/ppermute | solution.py:226
  70.2 1.7 collective-permute-start.5
  72.5 24.2 %collective-permute-start.7 = (bf16[32,8192]{1,0:T(8,128)(2,1)}, bf16[32,8192]{1,0:T(8,128)(2,1)}, u32[]{:S(2)}, u32[]{:S(2)}) collective-permute-start(bf16[32,8192]{1,0:T(8,128)(2,1)} %get-tuple-element.22), channel_id=1, source_target_pairs={{0,1},{1,2},{2,3},{4,5},{5,6},{6,7},{8,9},{9,10},{10,11},{12,13},{... | collective-permute-start | bytes 1572872 | tf_op jit(solution)/shard_map/ppermute | solution.py:244
  93.2 17.0 %collective-permute-start.8 = (bf16[32,8192]{1,0:T(8,128)(2,1)}, bf16[32,8192]{1,0:T(8,128)(2,1)}, u32[]{:S(2)}, u32[]{:S(2)}) collective-permute-start(bf16[32,8192]{1,0:T(8,128)(2,1)} %get-tuple-element.22), channel_id=1, source_target_pairs={{3,2},{2,1},{1,0},{7,6},{6,5},{5,4},{11,10},{10,9},{9,8},{15,14},{... | collective-permute-start | bytes 1572872 | tf_op jit(solution)/shard_map/ppermute | solution.py:244
  94.5 17.0 %collective-permute-start.16 = (bf16[2,96,1024]{2,1,0:T(8,128)(2,1)}, bf16[2,96,1024]{2,1,0:T(8,128)(2,1)S(1)}, u32[]{:S(2)}, u32[]{:S(2)}) collective-permute-start(bf16[2,96,1024]{2,1,0:T(8,128)(2,1)} %get-tuple-element.15.refs_10_), channel_id=1, source_target_pairs={{0,4},{4,0},{8,12},{12,8},{16,20},{20,16},{24,28},{28,24},{1,5},{5... | collective-permute-start | bytes 1179656 | tf_op jit(solution)/shard_map/ppermute | solution.py:226
  94.6 19.3 %copy-start.37 = (bf16[32,8192]{1,0:T(8,128)(2,1)}, bf16[32,8192]{1,0:T(8,128)(2,1)S(1)}, u32[]{:S(2)}) copy-start(bf16[32,8192]{1,0:T(8,128)(2,1)S(1)} %collective-permute-done.29.refs_2_) | copy-start | bytes 1572868
  94.6 21.5 %collective-permute-start.31 = (bf16[32,8192]{1,0:T(8,128)(2,1)S(1)}, bf16[32,8192]{1,0:T(8,128)(2,1)S(1)}, u32[]{:S(2)}, u32[]{:S(2)}) collective-permute-start(bf16[32,8192]{1,0:T(8,128)(2,1)S(1)} %collective-permute-done.29.refs_2_), channel_id=1, source_target_pairs={{2,3},{6,7},{10,11},{14,15},{18,19},{22,23},{26,27},{30,31}} | collective-permute-start | bytes 1572872 | tf_op jit(solution)/shard_map/ppermute | solution.py:244
  95.4 20.8 %copy-start.38 = (bf16[32,8192]{1,0:T(8,128)(2,1)}, bf16[32,8192]{1,0:T(8,128)(2,1)S(1)}, u32[]{:S(2)}) copy-start(bf16[32,8192]{1,0:T(8,128)(2,1)S(1)} %collective-permute-done.30.refs_3_) | copy-start | bytes 1572868
  95.4 26.0 %collective-permute-start.32 = (bf16[32,8192]{1,0:T(8,128)(2,1)S(1)}, bf16[32,8192]{1,0:T(8,128)(2,1)S(1)}, u32[]{:S(2)}, u32[]{:S(2)}) collective-permute-start(bf16[32,8192]{1,0:T(8,128)(2,1)S(1)} %collective-permute-done.30.refs_3_), channel_id=1, source_target_pairs={{1,0},{5,4},{9,8},{13,12},{17,16},{21,20},{25,24},{29,28}} | collective-permute-start | bytes 1572872 | tf_op jit(solution)/shard_map/ppermute | solution.py:244
  96.7 33.1 %collective-permute-start.9 = (bf16[32,8192]{1,0:T(8,128)(2,1)}, bf16[32,8192]{1,0:T(8,128)(2,1)}, u32[]{:S(2)}, u32[]{:S(2)}) collective-permute-start(bf16[32,8192]{1,0:T(8,128)(2,1)} %collective-permute-done.7.refs_0_), channel_id=1, source_target_pairs={{1,2},{2,3},{5,6},{6,7},{9,10},{10,11},{13,14},{14,15},{17,18},{18... | collective-permute-start | bytes 1572872 | tf_op jit(solution)/shard_map/ppermute | solution.py:244
  110.2 21.0 %collective-permute-start.10 = (bf16[32,8192]{1,0:T(8,128)(2,1)}, bf16[32,8192]{1,0:T(8,128)(2,1)}, u32[]{:S(2)}, u32[]{:S(2)}) collective-permute-start(bf16[32,8192]{1,0:T(8,128)(2,1)} %collective-permute-done.8.refs_1_), channel_id=1, source_target_pairs={{2,1},{1,0},{6,5},{5,4},{10,9},{9,8},{14,13},{13,12},{18,17},{17,1... | collective-permute-start | bytes 1572872 | tf_op jit(solution)/shard_map/ppermute | solution.py:244
  112.3 1.7 collective-permute-start.6
  114.6 17.9 %collective-permute-start.15 = (bf16[2,96,1024]{2,1,0:T(8,128)(2,1)}, bf16[2,96,1024]{2,1,0:T(8,128)(2,1)}, u32[]{:S(2)}, u32[]{:S(2)}) collective-permute-start(bf16[2,96,1024]{2,1,0:T(8,128)(2,1)} %collective-permute-done.13.refs_11_), channel_id=1, source_target_pairs={{0,16},{4,12},{8,24},{12,4},{16,0},{20,28},{24,8},{28,20},{1,17},{... | collective-permute-start | bytes 1179656 | tf_op jit(solution)/shard_map/ppermute | solution.py:226
  116.1 16.9 %collective-permute-start.17 = (bf16[2,96,1024]{2,1,0:T(8,128)(2,1)}, bf16[2,96,1024]{2,1,0:T(8,128)(2,1)}, u32[]{:S(2)}, u32[]{:S(2)}) collective-permute-start(bf16[2,96,1024]{2,1,0:T(8,128)(2,1)} %collective-permute-done.13.refs_11_), channel_id=1, source_target_pairs={{0,4},{4,0},{8,12},{12,8},{16,20},{20,16},{24,28},{28,24},{1,5},{5... | collective-permute-start | bytes 1179656 | tf_op jit(solution)/shard_map/ppermute | solution.py:226
  122.2 12.4 %collective-permute-start.18 = (bf16[2,96,1024]{2,1,0:T(8,128)(2,1)}, bf16[2,96,1024]{2,1,0:T(8,128)(2,1)}, u32[]{:S(2)}, u32[]{:S(2)}) collective-permute-start(bf16[2,96,1024]{2,1,0:T(8,128)(2,1)} %collective-permute-done.14.refs_12_), channel_id=1, source_target_pairs={{0,4},{4,0},{8,12},{12,8},{16,20},{20,16},{24,28},{28,24},{1,5},{5... | collective-permute-start | bytes 1179656 | tf_op jit(solution)/shard_map/ppermute | solution.py:226
  125.4 51.8 %all-to-all-start.2 = ((bf16[8,96,1024]{2,1,0:T(8,128)(2,1)}), bf16[8,96,1024]{2,1,0:T(8,128)(2,1)}, u32[]{:S(2)}, u32[]{:S(2)}) async-start(bf16[8,96,1024]{2,1,0:T(8,128)(2,1)} %get-tuple-element.17), calls=%async_computation.2 | async-start | bytes 3145728 | tf_op jit(solution)/shard_map/all_to_all | solution.py:240
  129.8 7.1 %collective-permute-start.11 = (bf16[32,8192]{1,0:T(8,128)(2,1)}, bf16[32,8192]{1,0:T(8,128)(2,1)}, u32[]{:S(2)}, u32[]{:S(2)}) collective-permute-start(bf16[32,8192]{1,0:T(8,128)(2,1)} %collective-permute-done.9.refs_2_), channel_id=1, source_target_pairs={{2,3},{6,7},{10,11},{14,15},{18,19},{22,23},{26,27},{30,31}} | collective-permute-start | bytes 1572872 | tf_op jit(solution)/shard_map/ppermute | solution.py:244
  131.2 16.5 %collective-permute-start.12 = (bf16[32,8192]{1,0:T(8,128)(2,1)}, bf16[32,8192]{1,0:T(8,128)(2,1)}, u32[]{:S(2)}, u32[]{:S(2)}) collective-permute-start(bf16[32,8192]{1,0:T(8,128)(2,1)} %collective-permute-done.10.refs_3_), channel_id=1, source_target_pairs={{1,0},{5,4},{9,8},{13,12},{17,16},{21,20},{25,24},{29,28}} | collective-permute-start | bytes 1572872 | tf_op jit(solution)/shard_map/ppermute | solution.py:244
  132.5 3.6 %collective-permute-start.19 = (bf16[2,96,1024]{2,1,0:T(8,128)(2,1)}, bf16[2,96,1024]{2,1,0:T(8,128)(2,1)S(1)}, u32[]{:S(2)}, u32[]{:S(2)}) collective-permute-start(bf16[2,96,1024]{2,1,0:T(8,128)(2,1)} %collective-permute-done.15.refs_13_), channel_id=1, source_target_pairs={{0,4},{4,0},{8,12},{12,8},{16,20},{20,16},{24,28},{28,24},{1,5},{5... | collective-permute-start | bytes 1179656 | tf_op jit(solution)/shard_map/ppermute | solution.py:226
  133.0 25.8 %collective-permute-start.46 = (bf16[2,96,1024]{2,1,0:T(8,128)(2,1)}, bf16[2,96,1024]{2,1,0:T(8,128)(2,1)}, u32[]{:S(2)}, u32[]{:S(2)}) collective-permute-start(bf16[2,96,1024]{2,1,0:T(8,128)(2,1)} %get-tuple-element.20.refs_18_), channel_id=1, source_target_pairs={{0,8},{4,20},{8,0},{12,28},{16,24},{20,4},{24,16},{28,12},{1,9},{5... | collective-permute-start | bytes 1179656 | tf_op jit(solution)/shard_map/ppermute | solution.py:226
  134.6 24.3 %collective-permute-start.47 = (bf16[2,96,1024]{2,1,0:T(8,128)(2,1)}, bf16[2,96,1024]{2,1,0:T(8,128)(2,1)}, u32[]{:S(2)}, u32[]{:S(2)}) collective-permute-start(bf16[2,96,1024]{2,1,0:T(8,128)(2,1)} %get-tuple-element.20.refs_18_), channel_id=1, source_target_pairs={{0,16},{4,12},{8,24},{12,4},{16,0},{20,28},{24,8},{28,20},{1,17},{... | collective-permute-start | bytes 1179656 | tf_op jit(solution)/shard_map/ppermute | solution.py:226
  136.8 26.8 %collective-permute-start.49 = (bf16[2,96,1024]{2,1,0:T(8,128)(2,1)}, bf16[2,96,1024]{2,1,0:T(8,128)(2,1)}, u32[]{:S(2)}, u32[]{:S(2)}) collective-permute-start(bf16[2,96,1024]{2,1,0:T(8,128)(2,1)} %get-tuple-element.20.refs_18_), channel_id=1, source_target_pairs={{0,4},{4,0},{8,12},{12,8},{16,20},{20,16},{24,28},{28,24},{1,5},{5... | collective-permute-start | bytes 1179656 | tf_op jit(solution)/shard_map/ppermute | solution.py:226
  136.9 38.2 %copy-start.41 = (s32[8]{0:T(128)S(1)}, s32[8]{0:T(128)}, u32[]{:S(2)}) copy-start(s32[8]{0:T(128)} %constant.59.clone) | copy-start | bytes 100
  136.9 38.2 %copy-start.42 = (s32[8]{0:T(128)S(1)}, s32[8]{0:T(128)}, u32[]{:S(2)}) copy-start(s32[8]{0:T(128)} %constant.60.clone) | copy-start | bytes 100
  136.9 30.4 %collective-permute-start.33 = (bf16[2,96,1024]{2,1,0:T(8,128)(2,1)}, bf16[2,96,1024]{2,1,0:T(8,128)(2,1)}, u32[]{:S(2)}, u32[]{:S(2)}) collective-permute-start(bf16[2,96,1024]{2,1,0:T(8,128)(2,1)} %get-tuple-element.18.refs_18_), channel_id=1, source_target_pairs={{0,8},{4,20},{8,0},{12,28},{16,24},{20,4},{24,16},{28,12},{1,9},{5... | collective-permute-start | bytes 1179656 | tf_op jit(solution)/shard_map/ppermute | solution.py:226
  147.7 19.6 %collective-permute-start.34 = (bf16[2,96,1024]{2,1,0:T(8,128)(2,1)}, bf16[2,96,1024]{2,1,0:T(8,128)(2,1)}, u32[]{:S(2)}, u32[]{:S(2)}) collective-permute-start(bf16[2,96,1024]{2,1,0:T(8,128)(2,1)} %get-tuple-element.18.refs_18_), channel_id=1, source_target_pairs={{0,16},{4,12},{8,24},{12,4},{16,0},{20,28},{24,8},{28,20},{1,17},{... | collective-permute-start | bytes 1179656 | tf_op jit(solution)/shard_map/ppermute | solution.py:226
  158.9 8.9 %collective-permute-start.36 = (bf16[2,96,1024]{2,1,0:T(8,128)(2,1)}, bf16[2,96,1024]{2,1,0:T(8,128)(2,1)}, u32[]{:S(2)}, u32[]{:S(2)}) collective-permute-start(bf16[2,96,1024]{2,1,0:T(8,128)(2,1)} %get-tuple-element.18.refs_18_), channel_id=1, source_target_pairs={{0,4},{4,0},{8,12},{12,8},{16,20},{20,16},{24,28},{28,24},{1,5},{5... | collective-permute-start | bytes 1179656 | tf_op jit(solution)/shard_map/ppermute | solution.py:226
  158.9 16.2 %collective-permute-start.48 = (bf16[2,96,1024]{2,1,0:T(8,128)(2,1)}, bf16[2,96,1024]{2,1,0:T(8,128)(2,1)}, u32[]{:S(2)}, u32[]{:S(2)}) collective-permute-start(bf16[2,96,1024]{2,1,0:T(8,128)(2,1)} %collective-permute-done.46.refs_19_), channel_id=1, source_target_pairs={{0,16},{4,12},{8,24},{12,4},{16,0},{20,28},{24,8},{28,20},{1,17},{... | collective-permute-start | bytes 1179656 | tf_op jit(solution)/shard_map/ppermute | solution.py:226
  163.7 12.3 %collective-permute-start.20 = (bf16[2,96,1024]{2,1,0:T(8,128)(2,1)}, bf16[2,96,1024]{2,1,0:T(8,128)(2,1)}, u32[]{:S(2)}, u32[]{:S(2)}) collective-permute-start(bf16[2,96,1024]{2,1,0:T(8,128)(2,1)} %get-tuple-element.16.refs_18_), channel_id=1, source_target_pairs={{0,8},{4,20},{8,0},{12,28},{16,24},{20,4},{24,16},{28,12},{1,9},{5... | collective-permute-start | bytes 1179656 | tf_op jit(solution)/shard_map/ppermute | solution.py:226
  167.3 14.4 %collective-permute-start.50 = (bf16[2,96,1024]{2,1,0:T(8,128)(2,1)}, bf16[2,96,1024]{2,1,0:T(8,128)(2,1)}, u32[]{:S(2)}, u32[]{:S(2)}) collective-permute-start(bf16[2,96,1024]{2,1,0:T(8,128)(2,1)} %collective-permute-done.46.refs_19_), channel_id=1, source_target_pairs={{0,4},{4,0},{8,12},{12,8},{16,20},{20,16},{24,28},{28,24},{1,5},{5... | collective-permute-start | bytes 1179656 | tf_op jit(solution)/shard_map/ppermute | solution.py:226
  167.3 14.6 %collective-permute-start.51 = (bf16[2,96,1024]{2,1,0:T(8,128)(2,1)}, bf16[2,96,1024]{2,1,0:T(8,128)(2,1)}, u32[]{:S(2)}, u32[]{:S(2)}) collective-permute-start(bf16[2,96,1024]{2,1,0:T(8,128)(2,1)} %collective-permute-done.47.refs_20_), channel_id=1, source_target_pairs={{0,4},{4,0},{8,12},{12,8},{16,20},{20,16},{24,28},{28,24},{1,5},{5... | collective-permute-start | bytes 1179656 | tf_op jit(solution)/shard_map/ppermute | solution.py:226
  167.8 14.5 %collective-permute-start.35 = (bf16[2,96,1024]{2,1,0:T(8,128)(2,1)}, bf16[2,96,1024]{2,1,0:T(8,128)(2,1)}, u32[]{:S(2)}, u32[]{:S(2)}) collective-permute-start(bf16[2,96,1024]{2,1,0:T(8,128)(2,1)} %collective-permute-done.33.refs_19_), channel_id=1, source_target_pairs={{0,16},{4,12},{8,24},{12,4},{16,0},{20,28},{24,8},{28,20},{1,17},{... | collective-permute-start | bytes 1179656 | tf_op jit(solution)/shard_map/ppermute | solution.py:226
  175.1 8.9 %collective-permute-start.52 = (bf16[2,96,1024]{2,1,0:T(8,128)(2,1)}, bf16[2,96,1024]{2,1,0:T(8,128)(2,1)}, u32[]{:S(2)}, u32[]{:S(2)}) collective-permute-start(bf16[2,96,1024]{2,1,0:T(8,128)(2,1)} %collective-permute-done.48.refs_21_), channel_id=1, source_target_pairs={{0,4},{4,0},{8,12},{12,8},{16,20},{20,16},{24,28},{28,24},{1,5},{5... | collective-permute-start | bytes 1179656 | tf_op jit(solution)/shard_map/ppermute | solution.py:226
  176.0 30.5 %collective-permute-start.21 = (bf16[2,96,1024]{2,1,0:T(8,128)(2,1)}, bf16[2,96,1024]{2,1,0:T(8,128)(2,1)}, u32[]{:S(2)}, u32[]{:S(2)}) collective-permute-start(bf16[2,96,1024]{2,1,0:T(8,128)(2,1)} %get-tuple-element.16.refs_18_), channel_id=1, source_target_pairs={{0,16},{4,12},{8,24},{12,4},{16,0},{20,28},{24,8},{28,20},{1,17},{... | collective-permute-start | bytes 1179656 | tf_op jit(solution)/shard_map/ppermute | solution.py:226
  177.2 50.6 %all-to-all-start.1 = ((bf16[8,96,1024]{2,1,0:T(8,128)(2,1)}), bf16[8,96,1024]{2,1,0:T(8,128)(2,1)}, u32[]{:S(2)}, u32[]{:S(2)}) async-start(bf16[8,96,1024]{2,1,0:T(8,128)(2,1)} %get-tuple-element.14), calls=%async_computation.1 | async-start | bytes 3145728 | tf_op jit(solution)/shard_map/all_to_all | solution.py:240
  181.7 25.4 %collective-permute-start.37 = (bf16[2,96,1024]{2,1,0:T(8,128)(2,1)}, bf16[2,96,1024]{2,1,0:T(8,128)(2,1)S(1)}, u32[]{:S(2)}, u32[]{:S(2)}) collective-permute-start(bf16[2,96,1024]{2,1,0:T(8,128)(2,1)} %collective-permute-done.33.refs_19_), channel_id=1, source_target_pairs={{0,4},{4,0},{8,12},{12,8},{16,20},{20,16},{24,28},{28,24},{1,5},{5... | collective-permute-start | bytes 1179656 | tf_op jit(solution)/shard_map/ppermute | solution.py:226
  181.9 25.3 %collective-permute-start.38 = (bf16[2,96,1024]{2,1,0:T(8,128)(2,1)}, bf16[2,96,1024]{2,1,0:T(8,128)(2,1)S(1)}, u32[]{:S(2)}, u32[]{:S(2)}) collective-permute-start(bf16[2,96,1024]{2,1,0:T(8,128)(2,1)} %collective-permute-done.34.refs_20_), channel_id=1, source_target_pairs={{0,4},{4,0},{8,12},{12,8},{16,20},{20,16},{24,28},{28,24},{1,5},{5... | collective-permute-start | bytes 1179656 | tf_op jit(solution)/shard_map/ppermute | solution.py:226
  182.3 25.3 %collective-permute-start.22 = (bf16[2,96,1024]{2,1,0:T(8,128)(2,1)}, bf16[2,96,1024]{2,1,0:T(8,128)(2,1)S(1)}, u32[]{:S(2)}, u32[]{:S(2)}) collective-permute-start(bf16[2,96,1024]{2,1,0:T(8,128)(2,1)} %collective-permute-done.20.refs_19_), channel_id=1, source_target_pairs={{0,16},{4,12},{8,24},{12,4},{16,0},{20,28},{24,8},{28,20},{1,17},{... | collective-permute-start | bytes 1179656 | tf_op jit(solution)/shard_map/ppermute | solution.py:226
  184.0 23.7 %collective-permute-start.39 = (bf16[2,96,1024]{2,1,0:T(8,128)(2,1)}, bf16[2,96,1024]{2,1,0:T(8,128)(2,1)S(1)}, u32[]{:S(2)}, u32[]{:S(2)}) collective-permute-start(bf16[2,96,1024]{2,1,0:T(8,128)(2,1)} %collective-permute-done.35.refs_21_), channel_id=1, source_target_pairs={{0,4},{4,0},{8,12},{12,8},{16,20},{20,16},{24,28},{28,24},{1,5},{5... | collective-permute-start | bytes 1179656 | tf_op jit(solution)/shard_map/ppermute | solution.py:226
  206.5 18.3 %collective-permute-start.23 = (bf16[2,96,1024]{2,1,0:T(8,128)(2,1)S(1)}, bf16[2,96,1024]{2,1,0:T(8,128)(2,1)S(1)}, u32[]{:S(2)}, u32[]{:S(2)}) collective-permute-start(bf16[2,96,1024]{2,1,0:T(8,128)(2,1)S(1)} %copy-done.13), channel_id=1, source_target_pairs={{0,4},{4,0},{8,12},{12,8},{16,20},{20,16},{24,28},{28,24},{1,5},{5... | collective-permute-start | bytes 1179656 | tf_op jit(solution)/shard_map/ppermute | solution.py:226
  207.1 18.5 %collective-permute-start.24 = (bf16[2,96,1024]{2,1,0:T(8,128)(2,1)}, bf16[2,96,1024]{2,1,0:T(8,128)(2,1)S(1)}, u32[]{:S(2)}, u32[]{:S(2)}) collective-permute-start(bf16[2,96,1024]{2,1,0:T(8,128)(2,1)} %collective-permute-done.20.refs_19_), channel_id=1, source_target_pairs={{0,4},{4,0},{8,12},{12,8},{16,20},{20,16},{24,28},{28,24},{1,5},{5... | collective-permute-start | bytes 1179656 | tf_op jit(solution)/shard_map/ppermute | solution.py:226
  207.2 19.2 %collective-permute-start.25 = (bf16[2,96,1024]{2,1,0:T(8,128)(2,1)}, bf16[2,96,1024]{2,1,0:T(8,128)(2,1)S(1)}, u32[]{:S(2)}, u32[]{:S(2)}) collective-permute-start(bf16[2,96,1024]{2,1,0:T(8,128)(2,1)} %collective-permute-done.21.refs_20_), channel_id=1, source_target_pairs={{0,4},{4,0},{8,12},{12,8},{16,20},{20,16},{24,28},{28,24},{1,5},{5... | collective-permute-start | bytes 1179656 | tf_op jit(solution)/shard_map/ppermute | solution.py:226
  207.6 19.5 %collective-permute-start.26 = (bf16[2,96,1024]{2,1,0:T(8,128)(2,1)S(1)}, bf16[2,96,1024]{2,1,0:T(8,128)(2,1)S(1)}, u32[]{:S(2)}, u32[]{:S(2)}) collective-permute-start(bf16[2,96,1024]{2,1,0:T(8,128)(2,1)S(1)} %collective-permute-done.22.refs_21_), channel_id=1, source_target_pairs={{0,4},{4,0},{8,12},{12,8},{16,20},{20,16},{24,28},{28,24},{1,5},{5... | collective-permute-start | bytes 1179656 | tf_op jit(solution)/shard_map/ppermute | solution.py:226
  (37 other events, 135.8 us)
where the time goes:
time: 258 us; the launch traced here: 256 us
  waiting for transfers between devices  87.2 us (34%)
  starting transfers between devices  76.1 us (29%)
  Pallas kernels  62.2 us (24%)
  local copies, waits for them, and re-layouts  29.2 us (11%)
    pallas_call x3, Pallas kernels, update(): pl.pallas_call(body, grid_spec=pltpu.PrefetchScalarGridSpec(num_scalar_pr...  49.6 us
    ppermute x18, waiting for transfers between devices, along(): return lax.ppermute(v, 'par', pairs)  49.1 us
    ppermute x35, waiting for transfers between devices, hop(): return lax.ppermute(v, 'arc', moves)  38.1 us
    ppermute x18, starting transfers between devices, along(): return lax.ppermute(v, 'par', pairs)  35.3 us
    unnamed x88, local copies, waits for them, and re-layouts  25.8 us
    ppermute x35, starting transfers between devices, hop(): return lax.ppermute(v, 'arc', moves)  24.6 us
    all_to_all x4, starting transfers between devices, exchange(): lax.all_to_all(blocks, 'arc', split_axis=0, concat_axis=0, tiled=True)  16.2 us
    pallas_call x4, Pallas kernels, place(): pl.pallas_call(body, in_specs=[pl.BlockSpec(memory_space=pltpu.SMEM)] + [...  12.7 us
  transfers between devices with their start and end apart: 57, of which 14 were waited for; matrix products, arithmetic and copies ran while one was open for 1% of the time, Pallas kernels for 18%

commit v1 on v0

--- a/solution.py
+++ b/solution.py
@@ -104,71 +104,126 @@
     )(z.reshape(1), *arrays)
 
 
-def update(total, slots, gram, component, rows, columns, steps=4):
-    arcs, epochs = len(gram), gram[0].shape[-1]
-    components = gram[0].shape[0]
-    height = rows[0][0].shape[2]
-    parts, _, width = columns[0][0][0].shape
+def place_own(z, block, gram, blocks, share):
+    width = block.shape[1] // blocks
+    depth = block.shape[0]
+    count, epochs, _ = gram.shape
+    rest = depth // count
+
+    def body(z_ref, block_ref, gram_ref, out, part):
+        for i in range(blocks):
+            out[i] = block_ref[:, i * width : (i + 1) * width]
+        for i in range(share):
+            part[i] = out[z_ref[0] * share + i]
+        for c in range(count):
+            matrix = gram_ref[c]
+            high = matrix.astype(jnp.bfloat16)
+            low = (matrix - high.astype(jnp.float32)).astype(jnp.bfloat16)
+            at = slice(c * rest, (c + 1) * rest)
+            for half, value in enumerate((high, low)):
+                for q in range(epochs // rest):
+                    lane = (half * (epochs // rest) + q) * epochs
+                    part[share, at, lane : lane + epochs] = value[q * rest : (q + 1) * rest]
+
+    vmem = pl.BlockSpec(memory_space=pltpu.VMEM)
+    return pl.pallas_call(
+        body,
+        in_specs=[pl.BlockSpec(memory_space=pltpu.SMEM), vmem, vmem],
+        out_specs=[vmem, vmem],
+        out_shape=[
+            jax.ShapeDtypeStruct((blocks, depth, width), block.dtype),
+            jax.ShapeDtypeStruct((share + 1, depth, width), block.dtype),
+        ],
+        cost_estimate=pl.CostEstimate(
+            flops=0, bytes_accessed=4 * blocks * depth * width, transcendentals=0
+        ),
+        name="place_own",
+    )(z.reshape(1), block, gram)
+
+
+def update(total, slots, components, epochs, work, steps=2):
+    gram = work[0][2][0][0]
+    arcs = len(gram)
+    height = work[0][1][0][0].shape[2]
+    _, whole_depth, width = gram[0].shape
+    parts = work[0][2][1][0][0].shape[0]
+    rest = whole_depth // components
     first = total is None
-    sizes = [v.shape[1] if at is None else v.shape[1] // components for v, at in rows]
-    count = len(rows)
+    sizes = [
+        v.shape[1] if at is None else v.shape[1] // components for v, at in work[0][1]
+    ]
+    count = len(sizes)
     tile = height // steps
     depth = arcs * epochs
+    whole_k = depth * len(work)
 
     def body(slot_ref, *refs):
         gram_refs, refs = refs[:arcs], refs[arcs:]
-        row_refs, refs = refs[:count], refs[count:]
-        col_refs, refs = refs[: count * arcs], refs[count * arcs :]
-        out_ref, high_ref, low_ref, col_all = refs[-4:]
+        row_refs, refs = refs[: count * len(work)], refs[count * len(work) :]
+        col_refs, refs = refs[: count * arcs * len(work)], refs[count * arcs * len(work) :]
+        out_ref, mixed_ref, col_all = refs[-3:]
         n, m = pl.program_id(0), pl.program_id(1)
 
         @pl.when((n == 0) & (m == 0))
         def _():
-            for slot in range(arcs):
-                arc = slot_ref[slot]
-                piece = jnp.concatenate([r[arc] for r in row_refs], axis=0)
-                matrix = gram_refs[slot][0]
-                high = matrix.astype(jnp.bfloat16)
-                low = (matrix - high.astype(jnp.float32)).astype(jnp.bfloat16)
-                both = jnp.concatenate([high, low], axis=0)
-                contract = (((0,), (1,)), ((), ()))
-                mixed = lax.dot_general(piece, both, contract, preferred_element_type=jnp.float32)
-                mixed = mixed[:, :epochs] + mixed[:, epochs:]
-                head = mixed.astype(jnp.bfloat16)
-                at = slice(slot * epochs, (slot + 1) * epochs)
-                high_ref[:, at] = head
-                low_ref[:, at] = (mixed - head.astype(jnp.float32)).astype(jnp.bfloat16)
+            for index in range(len(work)):
+                for slot in range(arcs):
+                    arc = slot_ref[slot]
+                    own = row_refs[index * count : (index + 1) * count]
+                    piece = jnp.concatenate([r[arc] for r in own], axis=0)
+                    both = [
+                        gram_refs[slot][0, :, q * epochs : (q + 1) * epochs]
+                        for q in range(2 * epochs // rest)
+                    ]
+                    both = jnp.concatenate(both, axis=0)
+                    contract = (((0,), (1,)), ((), ()))
+                    mixed = lax.dot_general(
+                        piece, both, contract, preferred_element_type=jnp.float32
+                    )
+                    mixed = mixed[:, :epochs] + mixed[:, epochs:]
+                    head = mixed.astype(jnp.bfloat16)
+                    tail = (mixed - head.astype(jnp.float32)).astype(jnp.bfloat16)
+                    start = index * depth + slot * epochs
+                    for t in range(steps):
+                        span = slice(t * tile, (t + 1) * tile)
+                        mixed_ref[t, :tile, start : start + epochs] = head[span]
+                        mixed_ref[t, tile:, start : start + epochs] = tail[span]
 
         @pl.when(m == 0)
         def _():
-            for slot in range(arcs):
-                start = slot * epochs
-                for i, size in enumerate(sizes):
-                    col_all[start : start + size, :] = col_refs[i * arcs + slot][0]
-                    start += size
-
-        span = pl.ds(pl.multiple_of(m * tile, tile), tile)
-        value = jnp.dot(high_ref[span, :], col_all[...], preferred_element_type=jnp.float32)
-        value = value + jnp.dot(low_ref[span, :], col_all[...], preferred_element_type=jnp.float32)
+            for index in range(len(work)):
+                for slot in range(arcs):
+                    start = index * depth + slot * epochs
+                    for i, size in enumerate(sizes):
+                        piece = col_refs[(index * count + i) * arcs + slot]
+                        col_all[start : start + size, :] = piece[0]
+                        start += size
+
+        value = jnp.dot(mixed_ref[m], col_all[...], preferred_element_type=jnp.float32)
+        value = value[:tile] + value[tile:]
         if first:
             out_ref[...] = value
         else:
             out_ref[...] = refs[0][...] + value
 
     args = list(gram)
-    in_specs = [pl.BlockSpec((1, epochs, epochs), lambda n, m, _: (component, 0, 0))] * arcs
-    for (v, at), size in zip(rows, sizes):
-        block = 0 if at is None else at
-        args.append(v)
-        in_specs.append(
-            pl.BlockSpec((arcs, size, height), lambda n, m, _, block=block: (0, block, 0))
-        )
-    for (arrays, at), size in zip(columns, sizes):
-        block = 0 if at is None else at
-        args.extend(arrays)
-        in_specs.extend(
-            [pl.BlockSpec((1, size, width), lambda n, m, _, block=block: (n, block, 0))] * arcs
-        )
+    place_at = work[0][0]
+    in_specs = [pl.BlockSpec((1, rest, width), lambda n, m, _: (parts, place_at, 0))] * arcs
+    for _, rows, _ in work:
+        for (v, at), size in zip(rows, sizes):
+            block = 0 if at is None else at
+            args.append(v)
+            in_specs.append(
+                pl.BlockSpec((arcs, size, height), lambda n, m, _, block=block: (0, block, 0))
+            )
+    for _, _, columns in work:
+        for (arrays, at), size in zip(columns, sizes):
+            block = 0 if at is None else at
+            args.extend(arrays)
+            in_specs.extend(
+                [pl.BlockSpec((1, size, width), lambda n, m, _, block=block: (n, block, 0))] * arcs
+            )
+    args = [pltpu.with_memory_space_constraint(v, pltpu.HBM) for v in args]
     whole = pl.BlockSpec((tile, width), lambda n, m, _: (m, n))
     aliases = {}
     if not first:
@@ -183,16 +238,17 @@
             in_specs=in_specs,
             out_specs=whole,
             scratch_shapes=[
-                pltpu.VMEM((height, depth), jnp.bfloat16),
-                pltpu.VMEM((height, depth), jnp.bfloat16),
-                pltpu.VMEM((depth, width), jnp.bfloat16),
+                pltpu.VMEM((steps, 2 * tile, whole_k), jnp.bfloat16),
+                pltpu.VMEM((whole_k, width), jnp.bfloat16),
             ],
         ),
         out_shape=jax.ShapeDtypeStruct((height, parts * width), jnp.float32),
         input_output_aliases=aliases,
-        compiler_params=pltpu.CompilerParams(vmem_limit_bytes=24 * 1024 * 1024),
+        compiler_params=pltpu.CompilerParams(
+            vmem_limit_bytes=32 * 1024 * 1024
+        ),
         cost_estimate=pl.CostEstimate(
-            flops=4 * height * parts * width * depth,
+            flops=4 * height * parts * width * whole_k,
             bytes_accessed=8 * height * parts * width,
             transcendentals=0,
         ),
@@ -258,9 +314,8 @@
     share = arc_count // par_count
 
     own = partials.reshape(components * epoch_block, param_count)
-    blocks, part = place(z, [own], [[(lambda i: i >= 0, 0)]], arc_count, share)
+    blocks, part = place_own(z, own, gram, arc_count, share)
     own_rows, own_columns = exchange(blocks, part)
-    grams = in_plane(gram)
     total = None
     for c in range(components):
         up = [own[c * epoch_block : (c + 1) * epoch_block]]
@@ -271,12 +326,14 @@
             pairs = [(par_count - 1 - i, par_count - 1 - j) for i, j in pairs]
             down.append(along(pairs, down[-1]))
         arrived = [v for both in zip(up[1:], down[1:]) for v in both]
-        blocks, part = place(z, arrived, [pick1, pick2, pick3], arc_count, share)
-        rows, columns = exchange(blocks, part)
-        total = update(
-            total, slots, grams, c, [(own_rows, c), (rows, None)],
-            [(own_columns, c), (columns, None)],
-        )
+        stages = [(arrived, [pick1, pick2, pick3])]
+        rows, columns = [(own_rows, c)], [(own_columns, c)]
+        for arrays, picks in stages:
+            blocks, part = place(z, arrays, picks, arc_count, share)
+            new_rows, new_columns = exchange(blocks, part)
+            rows.append((new_rows, None))
+            columns.append((new_columns, None))
+        total = update(total, slots, components, epochs, [(c, rows, columns)])
     return total
 
 

time: 258 us -> 233 us (0.903)
  local copies, waits for them, and re-layouts: 29.2 us -> 9.49 us
  starting transfers between devices: 76.1 us -> 65.6 us
  waiting for transfers between devices: 87.2 us -> 90.4 us
    unnamed x88 -> x74, local copies, waits for them, and re-layouts: 25.8 us -> 6.24 us
    ppermute x35 -> x28, starting transfers between devices: 24.6 us -> 16.3 us  [hop(): return lax.ppermute(v, 'arc', moves)]
    ppermute x35 -> x28, waiting for transfers between devices: 38.1 us -> 41.2 us  [hop(): return lax.ppermute(v, 'arc', moves)]
    pallas_call x0 -> x1, Pallas kernels: none -> 2.89 us  [place_own(): pl.pallas_call(body, in_specs=[pl.BlockSpec(memory_space=pltpu.SMEM), vme...]
    pallas_call x4 -> x3, Pallas kernels: 12.7 us -> 9.86 us  [place(): pl.pallas_call(body, in_specs=[pl.BlockSpec(memory_space=pltpu.SMEM)] + [...]
  transfers between devices with their start and end apart: 57 -> 50, of which waited for: 14 -> 14; matrix products, arithmetic and copies ran while one was open for 1% -> 1% of each run, Pallas kernels for 18% -> 20%
where the time goes in v1:
time: 233 us; the launch traced here: 230 us
  waiting for transfers between devices  90.4 us (39%)
  starting transfers between devices  65.6 us (28%)
  Pallas kernels  62.1 us (27%)
  local copies, waits for them, and re-layouts  9.49 us (4%)
    pallas_call x3, Pallas kernels, update(): pl.pallas_call(body, grid_spec=pltpu.PrefetchScalarGridSpec(num_scalar_pr...  49.3 us
    ppermute x18, waiting for transfers between devices, along(): return lax.ppermute(v, 'par', pairs)  49.1 us
    ppermute x28, waiting for transfers between devices, hop(): return lax.ppermute(v, 'arc', moves)  41.2 us
    ppermute x18, starting transfers between devices, along(): return lax.ppermute(v, 'par', pairs)  32.9 us
    all_to_all x4, starting transfers between devices, exchange(): lax.all_to_all(blocks, 'arc', split_axis=0, concat_axis=0, tiled=True)  16.4 us
    ppermute x28, starting transfers between devices, hop(): return lax.ppermute(v, 'arc', moves)  16.3 us
    pallas_call x3, Pallas kernels, place(): pl.pallas_call(body, in_specs=[pl.BlockSpec(memory_space=pltpu.SMEM)] + [...  9.86 us
    unnamed x74, local copies, waits for them, and re-layouts  6.24 us
  transfers between devices with their start and end apart: 50, of which 14 were waited for; matrix products, arithmetic and copies ran while one was open for 1% of the time, Pallas kernels for 20%

profile of v1, /device:TPU:0, one launch (start us, length us, event | category | flops | bytes accessed | tf_op | source)
XLA Modules:
  0.0 230.1 jit_solution(9244639420627107020)
XLA Ops:
  0.0 2.5 %slice_bitcast_fusion = (bf16[32,8192]{1,0:T(8,128)(2,1)}, bf16[32,8192]{1,0:T(8,128)(2,1)S(1)}, bf16[32,8192]{1,0:T(8,128)(2,1)}) fusion(bf16[1,3,32,8192]{3,2,1,0:T(8,128)(2,1)} %param.5), kind=kLoop, calls=%fused_computation.2 | loop fusion | bytes 3145728 | tf_op jit(solution)/shard_map/slice | solution.py:321
  2.5 5.0 %collective-permute-start.33 = (bf16[32,8192]{1,0:T(8,128)(2,1)}, bf16[32,8192]{1,0:T(8,128)(2,1)S(1)}, u32[]{:S(2)}, u32[]{:S(2)}) collective-permute-start(bf16[32,8192]{1,0:T(8,128)(2,1)} %get-tuple-element.21), channel_id=1, source_target_pairs={{0,1},{1,2},{2,3},{4,5},{5,6},{6,7},{8,9},{9,10},{10,11},{12,13},{... | collective-permute-start | bytes 1572872 | tf_op jit(solution)/shard_map/ppermute | solution.py:300
  7.5 1.3 collective-permute-start.34
  9.6 0.6 gather_fusion
  10.3 1.2 fusion.17.gram_ref
  11.5 2.9 %place_own.1 = (bf16[8,96,1024]{2,1,0:T(8,128)(2,1)}, bf16[3,96,1024]{2,1,0:T(8,128)(2,1)}) custom-call(s32[1]{0:T(128)} %bitcast.z_ref, bf16[96,8192]{1,0:T(8,128)(2,1)} %bitcast.35, f32[3,128,128]{2,1,0:T(8,128)} %fusion.17.gram_ref), custom_call_target="tpu_custom_call" | custom-call | bytes 3145728 | tf_op jit(solution)/shard_map/place_own/pallas_call | solution.py:129
  14.4 3.7 %all-to-all-start = ((bf16[8,96,1024]{2,1,0:T(8,128)(2,1)}), bf16[8,96,1024]{2,1,0:T(8,128)(2,1)S(1)}, u32[]{:S(2)}, u32[]{:S(2)}) async-start(bf16[8,96,1024]{2,1,0:T(8,128)(2,1)} %get-tuple-element.14), calls=%async_computation | async-start | bytes 3145728 | tf_op jit(solution)/shard_map/all_to_all | solution.py:296
  18.1 0.8 collective-permute-done.33.refs_0_
  18.9 0.7 collective-permute-start.35
  19.6 3.3 %collective-permute-done.34.refs_1_ = bf16[32,8192]{1,0:T(8,128)(2,1)S(1)} collective-permute-done((bf16[32,8192]{1,0:T(8,128)(2,1)}, bf16[32,8192]{1,0:T(8,128)(2,1)S(1)}, u32[]{:S(2)}, u32[]{:S(2)}) %collective-permute-start.34) | collective-permute-done | bytes 524320 | tf_op jit(solution)/shard_map/ppermute | solution.py:300
  23.0 1.3 collective-permute-start.36
  24.3 5.4 %collective-permute-start.20 = (bf16[32,8192]{1,0:T(8,128)(2,1)}, bf16[32,8192]{1,0:T(8,128)(2,1)}, u32[]{:S(2)}, u32[]{:S(2)}) collective-permute-start(bf16[32,8192]{1,0:T(8,128)(2,1)} %get-tuple-element.23), channel_id=1, source_target_pairs={{0,1},{1,2},{2,3},{4,5},{5,6},{6,7},{8,9},{9,10},{10,11},{12,13},{... | collective-permute-start | bytes 1572872 | tf_op jit(solution)/shard_map/ppermute | solution.py:300
  29.6 1.3 collective-permute-start.21
  30.9 0.7 collective-permute-start.37
  31.6 8.0 %collective-permute-done.36.refs_3_ = bf16[32,8192]{1,0:T(8,128)(2,1)S(1)} collective-permute-done((bf16[32,8192]{1,0:T(8,128)(2,1)S(1)}, bf16[32,8192]{1,0:T(8,128)(2,1)S(1)}, u32[]{:S(2)}, u32[]{:S(2)}) %collective-permute-start.36) | collective-permute-done | bytes 524320 | tf_op jit(solution)/shard_map/ppermute | solution.py:300
  39.7 1.3 collective-permute-start.38
  41.0 5.3 %collective-permute-start.7 = (bf16[32,8192]{1,0:T(8,128)(2,1)S(1)}, bf16[32,8192]{1,0:T(8,128)(2,1)S(1)}, u32[]{:S(2)}, u32[]{:S(2)}) collective-permute-start(bf16[32,8192]{1,0:T(8,128)(2,1)S(1)} %get-tuple-element.22), channel_id=1, source_target_pairs={{0,1},{1,2},{2,3},{4,5},{5,6},{6,7},{8,9},{9,10},{10,11},{12,13},{... | collective-permute-start | bytes 1572872 | tf_op jit(solution)/shard_map/ppermute | solution.py:300
  46.3 1.3 collective-permute-start.8
  47.6 3.4 %collective-permute-done.21.refs_1_ = bf16[32,8192]{1,0:T(8,128)(2,1)} collective-permute-done((bf16[32,8192]{1,0:T(8,128)(2,1)}, bf16[32,8192]{1,0:T(8,128)(2,1)}, u32[]{:S(2)}, u32[]{:S(2)}) %collective-permute-start.21) | collective-permute-done | bytes 524320 | tf_op jit(solution)/shard_map/ppermute | solution.py:300
  51.0 1.4 collective-permute-start.22
  52.5 1.3 collective-permute-start.23
  53.8 8.5 %collective-permute-done.38.refs_5_ = bf16[32,8192]{1,0:T(8,128)(2,1)} collective-permute-done((bf16[32,8192]{1,0:T(8,128)(2,1)S(1)}, bf16[32,8192]{1,0:T(8,128)(2,1)}, u32[]{:S(2)}, u32[]{:S(2)}) %collective-permute-start.38) | collective-permute-done | bytes 524320 | tf_op jit(solution)/shard_map/ppermute | solution.py:300
  62.2 3.3 %place.5 = (bf16[8,96,1024]{2,1,0:T(8,128)(2,1)}, bf16[2,96,1024]{2,1,0:T(8,128)(2,1)}) custom-call(s32[1]{0:T(128)} %bitcast.z_ref, bf16[32,8192]{1,0:T(8,128)(2,1)} %copy-done.11, bf16[32,8192]{1,0:T(8,128)(2,1)} %copy-done.12, bf16[32,8192]{1,0:T(8,128)(2,1)} %copy-done.14, bf16[32,8192]{1,0:T(8,128)(2,1)} %copy-done.16, bf16[32,8192]{1,0:T(8,128)(2,1)} %copy-done.18, ...), custom_call_target="tpu_custom_call" | custom-call | bytes 3145728 | tf_op jit(solution)/shard_map/place/pallas_call | solution.py:92
  65.6 1.1 copy-done.1
  66.7 4.3 %all-to-all-start.3 = ((bf16[8,96,1024]{2,1,0:T(8,128)(2,1)}), bf16[8,96,1024]{2,1,0:T(8,128)(2,1)}, u32[]{:S(2)}, u32[]{:S(2)}) async-start(bf16[8,96,1024]{2,1,0:T(8,128)(2,1)} %get-tuple-element.19), calls=%async_computation.3 | async-start | bytes 3145728 | tf_op jit(solution)/shard_map/all_to_all | solution.py:296
  71.0 1.9 collective-permute-start
  72.9 1.5 collective-permute-start.1
  74.5 0.7 collective-permute-start.24
  75.2 8.4 %collective-permute-done.23.refs_3_ = bf16[32,8192]{1,0:T(8,128)(2,1)} collective-permute-done((bf16[32,8192]{1,0:T(8,128)(2,1)}, bf16[32,8192]{1,0:T(8,128)(2,1)}, u32[]{:S(2)}, u32[]{:S(2)}) %collective-permute-start.23) | collective-permute-done | bytes 524320 | tf_op jit(solution)/shard_map/ppermute | solution.py:300
  83.5 1.3 collective-permute-start.25
  84.8 18.9 %collective-permute-done.refs_1_.refs_11_ = bf16[3,96,1024]{2,1,0:T(8,128)(2,1)S(1)} collective-permute-done((bf16[3,96,1024]{2,1,0:T(8,128)(2,1)S(1)}, bf16[3,96,1024]{2,1,0:T(8,128)(2,1)S(1)}, u32[]{:S(2)}, u32[]{:S(2)}) %collective-permute-start) | collective-permute-done | bytes 589856 | tf_op jit(solution)/shard_map/ppermute | solution.py:282
  103.7 1.5 collective-permute-start.2
  105.2 1.4 collective-permute-start.9
  106.6 1.3 collective-permute-start.10
  108.0 0.7 copy-done.17
  108.7 0.8 copy-done.19
  109.5 3.3 %place.4 = (bf16[8,96,1024]{2,1,0:T(8,128)(2,1)}, bf16[2,96,1024]{2,1,0:T(8,128)(2,1)}) custom-call(s32[1]{0:T(128)} %bitcast.z_ref, bf16[32,8192]{1,0:T(8,128)(2,1)} %collective-permute-done.20.refs_0_, bf16[32,8192]{1,0:T(8,128)(2,1)} %collective-permute-done.21.refs_1_, bf16[32,8192]{1,0:T(8,128)(2,1)} %collective-permute-done.22.refs_2_, ...), custom_call_target="tpu_custom_call" | custom-call | bytes 3145728 | tf_op jit(solution)/shard_map/place/pallas_call | solution.py:92
  112.8 4.4 %all-to-all-start.2 = ((bf16[8,96,1024]{2,1,0:T(8,128)(2,1)}), bf16[8,96,1024]{2,1,0:T(8,128)(2,1)}, u32[]{:S(2)}, u32[]{:S(2)}) async-start(bf16[8,96,1024]{2,1,0:T(8,128)(2,1)} %get-tuple-element.17), calls=%async_computation.2 | async-start | bytes 3145728 | tf_op jit(solution)/shard_map/all_to_all | solution.py:296
  117.3 0.5 collective-permute-start.6
  117.8 0.7 collective-permute-start.11
  118.5 4.0 %collective-permute-done.10.refs_3_ = bf16[32,8192]{1,0:T(8,128)(2,1)} collective-permute-done((bf16[32,8192]{1,0:T(8,128)(2,1)}, bf16[32,8192]{1,0:T(8,128)(2,1)}, u32[]{:S(2)}, u32[]{:S(2)}) %collective-permute-start.10) | collective-permute-done | bytes 524320 | tf_op jit(solution)/shard_map/ppermute | solution.py:300
  122.6 1.3 collective-permute-start.12
  124.7 12.7 %collective-permute-done.12.refs_5_ = bf16[32,8192]{1,0:T(8,128)(2,1)S(1)} collective-permute-done((bf16[32,8192]{1,0:T(8,128)(2,1)}, bf16[32,8192]{1,0:T(8,128)(2,1)S(1)}, u32[]{:S(2)}, u32[]{:S(2)}) %collective-permute-start.12) | collective-permute-done | bytes 524320 | tf_op jit(solution)/shard_map/ppermute | solution.py:300
  137.5 1.1 collective-permute-start.27
  138.5 7.9 %collective-permute-done.39.refs_19_ = bf16[2,96,1024]{2,1,0:T(8,128)(2,1)} collective-permute-done((bf16[2,96,1024]{2,1,0:T(8,128)(2,1)}, bf16[2,96,1024]{2,1,0:T(8,128)(2,1)}, u32[]{:S(2)}, u32[]{:S(2)}) %collective-permute-start.39) | collective-permute-done | bytes 393248 | tf_op jit(solution)/shard_map/ppermute | solution.py:282
  146.4 1.5 collective-permute-start.41
  147.9 3.3 %place.3 = (bf16[8,96,1024]{2,1,0:T(8,128)(2,1)}, bf16[2,96,1024]{2,1,0:T(8,128)(2,1)}) custom-call(s32[1]{0:T(128)} %bitcast.z_ref, bf16[32,8192]{1,0:T(8,128)(2,1)} %copy-done.10, bf16[32,8192]{1,0:T(8,128)(2,1)} %collective-permute-done.8.refs_1_, bf16[32,8192]{1,0:T(8,128)(2,1)} %collective-permute-done.9.refs_2_, ...), custom_call_target="tpu_custom_call" | custom-call | bytes 3145728 | tf_op jit(solution)/shard_map/place/pallas_call | solution.py:92
  151.2 0.6 collective-permute-start.13
  151.8 3.0 %collective-permute-done.26.refs_19_ = bf16[2,96,1024]{2,1,0:T(8,128)(2,1)} collective-permute-done((bf16[2,96,1024]{2,1,0:T(8,128)(2,1)S(1)}, bf16[2,96,1024]{2,1,0:T(8,128)(2,1)}, u32[]{:S(2)}, u32[]{:S(2)}) %collective-permute-start.26) | collective-permute-done | bytes 393248 | tf_op jit(solution)/shard_map/ppermute | solution.py:282
  155.3 1.5 collective-permute-start.28
  156.8 5.8 %collective-permute-done.41.refs_21_ = bf16[2,96,1024]{2,1,0:T(8,128)(2,1)} collective-permute-done((bf16[2,96,1024]{2,1,0:T(8,128)(2,1)}, bf16[2,96,1024]{2,1,0:T(8,128)(2,1)}, u32[]{:S(2)}, u32[]{:S(2)}) %collective-permute-start.41) | collective-permute-done | bytes 393248 | tf_op jit(solution)/shard_map/ppermute | solution.py:282
  162.6 0.8 collective-permute-done.13.refs_19_
  163.4 1.2 collective-permute-start.14
  164.6 3.9 %all-to-all-start.1 = ((bf16[8,96,1024]{2,1,0:T(8,128)(2,1)}), bf16[8,96,1024]{2,1,0:T(8,128)(2,1)S(1)}, u32[]{:S(2)}, u32[]{:S(2)}) async-start(bf16[8,96,1024]{2,1,0:T(8,128)(2,1)} %get-tuple-element.15), calls=%async_computation.1 | async-start | bytes 3145728 | tf_op jit(solution)/shard_map/all_to_all | solution.py:296
  169.2 1.7 collective-permute-start.15
  170.9 15.6 %update.3.refs_26_ = f32[1024,2048]{1,0:T(8,128)} custom-call(s32[8]{0:T(128)S(1)} %fusion.13.slot_ref, bf16[3,96,1024]{2,1,0:T(8,128)(2,1)} %get-tuple-element.13.refs_0_.refs_10_, bf16[3,96,1024]{2,1,0:T(8,128)(2,1)} %copy-done.3, bf16[3,96,1024]{2,1,0:T(8,128)(2,1)} %copy-done.4, bf16[3,96,1024]{2,1,0:T(8,128)(2,1)} %copy-done.6, ...), custom_call_target="tpu_custom_call" | custom-call | flops 8589934592 | bytes 16777216 | tf_op jit(solution)/shard_map/update/pallas_call | solution.py:233
  186.6 0.6 collective-permute-start.16
  187.7 4.8 %collective-permute-done.15.refs_21_ = bf16[2,96,1024]{2,1,0:T(8,128)(2,1)S(1)} collective-permute-done((bf16[2,96,1024]{2,1,0:T(8,128)(2,1)S(1)}, bf16[2,96,1024]{2,1,0:T(8,128)(2,1)S(1)}, u32[]{:S(2)}, u32[]{:S(2)}) %collective-permute-start.15) | collective-permute-done | bytes 393248 | tf_op jit(solution)/shard_map/ppermute | solution.py:282
  192.7 0.7 copy-done.33
  193.4 16.8 %update.4.refs_26_ = f32[1024,2048]{1,0:T(8,128)} custom-call(s32[8]{0:T(128)S(1)} %fusion.13.slot_ref, bf16[3,96,1024]{2,1,0:T(8,128)(2,1)} %get-tuple-element.13.refs_0_.refs_10_, bf16[3,96,1024]{2,1,0:T(8,128)(2,1)} %copy-done.3, bf16[3,96,1024]{2,1,0:T(8,128)(2,1)} %copy-done.4, bf16[3,96,1024]{2,1,0:T(8,128)(2,1)} %copy-done.6, ...), custom_call_target="tpu_custom_call", output_to_operand_aliasing={{}: (27, {})} | custom-call | flops 8589934592 | bytes 16777216 | tf_op jit(solution)/shard_map/update/pallas_call | solution.py:233
  210.3 0.7 copy-done.29
  211.2 0.8 copy-done.32
  212.0 1.1 copy-done.9
  213.1 16.8 %update.5 = f32[1024,2048]{1,0:T(8,128)} custom-call(s32[8]{0:T(128)S(1)} %fusion.13.slot_ref, bf16[3,96,1024]{2,1,0:T(8,128)(2,1)} %get-tuple-element.13.refs_0_.refs_10_, bf16[3,96,1024]{2,1,0:T(8,128)(2,1)} %copy-done.3, bf16[3,96,1024]{2,1,0:T(8,128)(2,1)} %copy-done.4, bf16[3,96,1024]{2,1,0:T(8,128)(2,1)} %copy-done.6, ...), custom_call_target="tpu_custom_call", output_to_operand_aliasing={{}: (27, {})} | custom-call | flops 8589934592 | bytes 16777216 | tf_op jit(solution)/shard_map/update/pallas_call | solution.py:233
  (130 shorter events, 4.0 us)
Async XLA Ops:
  2.5 16.4 %collective-permute-start.33 = (bf16[32,8192]{1,0:T(8,128)(2,1)}, bf16[32,8192]{1,0:T(8,128)(2,1)S(1)}, u32[]{:S(2)}, u32[]{:S(2)}) collective-permute-start(bf16[32,8192]{1,0:T(8,128)(2,1)} %get-tuple-element.21), channel_id=1, source_target_pairs={{0,1},{1,2},{2,3},{4,5},{5,6},{6,7},{8,9},{9,10},{10,11},{12,13},{... | collective-permute-start | bytes 1572872 | tf_op jit(solution)/shard_map/ppermute | solution.py:300
  7.5 15.5 %collective-permute-start.34 = (bf16[32,8192]{1,0:T(8,128)(2,1)}, bf16[32,8192]{1,0:T(8,128)(2,1)S(1)}, u32[]{:S(2)}, u32[]{:S(2)}) collective-permute-start(bf16[32,8192]{1,0:T(8,128)(2,1)} %get-tuple-element.21), channel_id=1, source_target_pairs={{3,2},{2,1},{1,0},{7,6},{6,5},{5,4},{11,10},{10,9},{9,8},{15,14},{... | collective-permute-start | bytes 1572872 | tf_op jit(solution)/shard_map/ppermute | solution.py:300
  14.4 51.2 %all-to-all-start = ((bf16[8,96,1024]{2,1,0:T(8,128)(2,1)}), bf16[8,96,1024]{2,1,0:T(8,128)(2,1)S(1)}, u32[]{:S(2)}, u32[]{:S(2)}) async-start(bf16[8,96,1024]{2,1,0:T(8,128)(2,1)} %get-tuple-element.14), calls=%async_computation | async-start | bytes 3145728 | tf_op jit(solution)/shard_map/all_to_all | solution.py:296
  18.9 43.3 %copy-start.11 = (bf16[32,8192]{1,0:T(8,128)(2,1)}, bf16[32,8192]{1,0:T(8,128)(2,1)S(1)}, u32[]{:S(2)}) copy-start(bf16[32,8192]{1,0:T(8,128)(2,1)S(1)} %collective-permute-done.33.refs_0_) | copy-start | bytes 1572868
  18.9 12.0 %collective-permute-start.35 = (bf16[32,8192]{1,0:T(8,128)(2,1)S(1)}, bf16[32,8192]{1,0:T(8,128)(2,1)S(1)}, u32[]{:S(2)}, u32[]{:S(2)}) collective-permute-start(bf16[32,8192]{1,0:T(8,128)(2,1)S(1)} %collective-permute-done.33.refs_0_), channel_id=1, source_target_pairs={{1,2},{2,3},{5,6},{6,7},{9,10},{10,11},{13,14},{14,15},{17,18},{18... | collective-permute-start | bytes 1572872 | tf_op jit(solution)/shard_map/ppermute | solution.py:300
  23.0 18.0 %copy-start.12 = (bf16[32,8192]{1,0:T(8,128)(2,1)}, bf16[32,8192]{1,0:T(8,128)(2,1)S(1)}, u32[]{:S(2)}) copy-start(bf16[32,8192]{1,0:T(8,128)(2,1)S(1)} %collective-permute-done.34.refs_1_) | copy-start | bytes 1572868
  23.0 16.7 %collective-permute-start.36 = (bf16[32,8192]{1,0:T(8,128)(2,1)S(1)}, bf16[32,8192]{1,0:T(8,128)(2,1)S(1)}, u32[]{:S(2)}, u32[]{:S(2)}) collective-permute-start(bf16[32,8192]{1,0:T(8,128)(2,1)S(1)} %collective-permute-done.34.refs_1_), channel_id=1, source_target_pairs={{2,1},{1,0},{6,5},{5,4},{10,9},{9,8},{14,13},{13,12},{18,17},{17,1... | collective-permute-start | bytes 1572872 | tf_op jit(solution)/shard_map/ppermute | solution.py:300
  24.3 22.0 %collective-permute-start.20 = (bf16[32,8192]{1,0:T(8,128)(2,1)}, bf16[32,8192]{1,0:T(8,128)(2,1)}, u32[]{:S(2)}, u32[]{:S(2)}) collective-permute-start(bf16[32,8192]{1,0:T(8,128)(2,1)} %get-tuple-element.23), channel_id=1, source_target_pairs={{0,1},{1,2},{2,3},{4,5},{5,6},{6,7},{8,9},{9,10},{10,11},{12,13},{... | collective-permute-start | bytes 1572872 | tf_op jit(solution)/shard_map/ppermute | solution.py:300
  29.6 21.4 %collective-permute-start.21 = (bf16[32,8192]{1,0:T(8,128)(2,1)}, bf16[32,8192]{1,0:T(8,128)(2,1)}, u32[]{:S(2)}, u32[]{:S(2)}) collective-permute-start(bf16[32,8192]{1,0:T(8,128)(2,1)} %get-tuple-element.23), channel_id=1, source_target_pairs={{3,2},{2,1},{1,0},{7,6},{6,5},{5,4},{11,10},{10,9},{9,8},{15,14},{... | collective-permute-start | bytes 1572872 | tf_op jit(solution)/shard_map/ppermute | solution.py:300
  30.9 16.7 %copy-start.14 = (bf16[32,8192]{1,0:T(8,128)(2,1)}, bf16[32,8192]{1,0:T(8,128)(2,1)S(1)}, u32[]{:S(2)}) copy-start(bf16[32,8192]{1,0:T(8,128)(2,1)S(1)} %collective-permute-done.35.refs_2_) | copy-start | bytes 1572868
  30.9 21.5 %collective-permute-start.37 = (bf16[32,8192]{1,0:T(8,128)(2,1)S(1)}, bf16[32,8192]{1,0:T(8,128)(2,1)S(1)}, u32[]{:S(2)}, u32[]{:S(2)}) collective-permute-start(bf16[32,8192]{1,0:T(8,128)(2,1)S(1)} %collective-permute-done.35.refs_2_), channel_id=1, source_target_pairs={{2,3},{6,7},{10,11},{14,15},{18,19},{22,23},{26,27},{30,31}} | collective-permute-start | bytes 1572872 | tf_op jit(solution)/shard_map/ppermute | solution.py:300
  39.7 22.6 %collective-permute-start.38 = (bf16[32,8192]{1,0:T(8,128)(2,1)S(1)}, bf16[32,8192]{1,0:T(8,128)(2,1)}, u32[]{:S(2)}, u32[]{:S(2)}) collective-permute-start(bf16[32,8192]{1,0:T(8,128)(2,1)S(1)} %collective-permute-done.36.refs_3_), channel_id=1, source_target_pairs={{1,0},{5,4},{9,8},{13,12},{17,16},{21,20},{25,24},{29,28}} | collective-permute-start | bytes 1572872 | tf_op jit(solution)/shard_map/ppermute | solution.py:300
  41.0 32.0 %collective-permute-start.7 = (bf16[32,8192]{1,0:T(8,128)(2,1)S(1)}, bf16[32,8192]{1,0:T(8,128)(2,1)S(1)}, u32[]{:S(2)}, u32[]{:S(2)}) collective-permute-start(bf16[32,8192]{1,0:T(8,128)(2,1)S(1)} %get-tuple-element.22), channel_id=1, source_target_pairs={{0,1},{1,2},{2,3},{4,5},{5,6},{6,7},{8,9},{9,10},{10,11},{12,13},{... | collective-permute-start | bytes 1572872 | tf_op jit(solution)/shard_map/ppermute | solution.py:300
  46.3 28.1 %collective-permute-start.8 = (bf16[32,8192]{1,0:T(8,128)(2,1)S(1)}, bf16[32,8192]{1,0:T(8,128)(2,1)}, u32[]{:S(2)}, u32[]{:S(2)}) collective-permute-start(bf16[32,8192]{1,0:T(8,128)(2,1)S(1)} %get-tuple-element.22), channel_id=1, source_target_pairs={{3,2},{2,1},{1,0},{7,6},{6,5},{5,4},{11,10},{10,9},{9,8},{15,14},{... | collective-permute-start | bytes 1572872 | tf_op jit(solution)/shard_map/ppermute | solution.py:300
  51.0 23.4 %collective-permute-start.22 = (bf16[32,8192]{1,0:T(8,128)(2,1)}, bf16[32,8192]{1,0:T(8,128)(2,1)}, u32[]{:S(2)}, u32[]{:S(2)}) collective-permute-start(bf16[32,8192]{1,0:T(8,128)(2,1)} %collective-permute-done.20.refs_0_), channel_id=1, source_target_pairs={{1,2},{2,3},{5,6},{6,7},{9,10},{10,11},{13,14},{14,15},{17,18},{18... | collective-permute-start | bytes 1572872 | tf_op jit(solution)/shard_map/ppermute | solution.py:300
  52.5 31.1 %collective-permute-start.23 = (bf16[32,8192]{1,0:T(8,128)(2,1)}, bf16[32,8192]{1,0:T(8,128)(2,1)}, u32[]{:S(2)}, u32[]{:S(2)}) collective-permute-start(bf16[32,8192]{1,0:T(8,128)(2,1)} %collective-permute-done.21.refs_1_), channel_id=1, source_target_pairs={{2,1},{1,0},{6,5},{5,4},{10,9},{9,8},{14,13},{13,12},{18,17},{17,1... | collective-permute-start | bytes 1572872 | tf_op jit(solution)/shard_map/ppermute | solution.py:300
  66.7 46.1 %all-to-all-start.3 = ((bf16[8,96,1024]{2,1,0:T(8,128)(2,1)}), bf16[8,96,1024]{2,1,0:T(8,128)(2,1)}, u32[]{:S(2)}, u32[]{:S(2)}) async-start(bf16[8,96,1024]{2,1,0:T(8,128)(2,1)} %get-tuple-element.19), calls=%async_computation.3 | async-start | bytes 3145728 | tf_op jit(solution)/shard_map/all_to_all | solution.py:296
  71.0 32.7 %collective-permute-start = (bf16[3,96,1024]{2,1,0:T(8,128)(2,1)S(1)}, bf16[3,96,1024]{2,1,0:T(8,128)(2,1)S(1)}, u32[]{:S(2)}, u32[]{:S(2)}) collective-permute-start(bf16[3,96,1024]{2,1,0:T(8,128)(2,1)S(1)} %copy-done.2), channel_id=1, source_target_pairs={{0,8},{4,20},{8,0},{12,28},{16,24},{20,4},{24,16},{28,12},{1,9},{5... | collective-permute-start | bytes 1769480 | tf_op jit(solution)/shard_map/ppermute | solution.py:282
  72.9 32.2 %collective-permute-start.1 = (bf16[3,96,1024]{2,1,0:T(8,128)(2,1)S(1)}, bf16[3,96,1024]{2,1,0:T(8,128)(2,1)S(1)}, u32[]{:S(2)}, u32[]{:S(2)}) collective-permute-start(bf16[3,96,1024]{2,1,0:T(8,128)(2,1)S(1)} %copy-done.2), channel_id=1, source_target_pairs={{0,16},{4,12},{8,24},{12,4},{16,0},{20,28},{24,8},{28,20},{1,17},{... | collective-permute-start | bytes 1769480 | tf_op jit(solution)/shard_map/ppermute | solution.py:282
  74.4 32.2 %collective-permute-start.3 = (bf16[3,96,1024]{2,1,0:T(8,128)(2,1)S(1)}, bf16[3,96,1024]{2,1,0:T(8,128)(2,1)S(1)}, u32[]{:S(2)}, u32[]{:S(2)}) collective-permute-start(bf16[3,96,1024]{2,1,0:T(8,128)(2,1)S(1)} %copy-done.2), channel_id=1, source_target_pairs={{0,4},{4,0},{8,12},{12,8},{16,20},{20,16},{24,28},{28,24},{1,5},{5... | collective-permute-start | bytes 1769480 | tf_op jit(solution)/shard_map/ppermute | solution.py:282
  74.5 33.5 %collective-permute-start.24 = (bf16[32,8192]{1,0:T(8,128)(2,1)}, bf16[32,8192]{1,0:T(8,128)(2,1)S(1)}, u32[]{:S(2)}, u32[]{:S(2)}) collective-permute-start(bf16[32,8192]{1,0:T(8,128)(2,1)} %collective-permute-done.22.refs_2_), channel_id=1, source_target_pairs={{2,3},{6,7},{10,11},{14,15},{18,19},{22,23},{26,27},{30,31}} | collective-permute-start | bytes 1572872 | tf_op jit(solution)/shard_map/ppermute | solution.py:300
  83.5 25.2 %collective-permute-start.25 = (bf16[32,8192]{1,0:T(8,128)(2,1)}, bf16[32,8192]{1,0:T(8,128)(2,1)S(1)}, u32[]{:S(2)}, u32[]{:S(2)}) collective-permute-start(bf16[32,8192]{1,0:T(8,128)(2,1)} %collective-permute-done.23.refs_3_), channel_id=1, source_target_pairs={{1,0},{5,4},{9,8},{13,12},{17,16},{21,20},{25,24},{29,28}} | collective-permute-start | bytes 1572872 | tf_op jit(solution)/shard_map/ppermute | solution.py:300
  103.7 13.6 %collective-permute-start.2 = (bf16[3,96,1024]{2,1,0:T(8,128)(2,1)S(1)}, bf16[3,96,1024]{2,1,0:T(8,128)(2,1)S(1)}, u32[]{:S(2)}, u32[]{:S(2)}) collective-permute-start(bf16[3,96,1024]{2,1,0:T(8,128)(2,1)S(1)} %collective-permute-done.refs_1_.refs_11_), channel_id=1, source_target_pairs={{0,16},{4,12},{8,24},{12,4},{16,0},{20,28},{24,8},{28,20},{1,17},{... | collective-permute-start | bytes 1769480 | tf_op jit(solution)/shard_map/ppermute | solution.py:282
  105.2 12.6 %collective-permute-start.9 = (bf16[32,8192]{1,0:T(8,128)(2,1)}, bf16[32,8192]{1,0:T(8,128)(2,1)}, u32[]{:S(2)}, u32[]{:S(2)}) collective-permute-start(bf16[32,8192]{1,0:T(8,128)(2,1)} %copy-done.10), channel_id=1, source_target_pairs={{1,2},{2,3},{5,6},{6,7},{9,10},{10,11},{13,14},{14,15},{17,18},{18... | collective-permute-start | bytes 1572872 | tf_op jit(solution)/shard_map/ppermute | solution.py:300
  106.6 15.9 %collective-permute-start.10 = (bf16[32,8192]{1,0:T(8,128)(2,1)}, bf16[32,8192]{1,0:T(8,128)(2,1)}, u32[]{:S(2)}, u32[]{:S(2)}) collective-permute-start(bf16[32,8192]{1,0:T(8,128)(2,1)} %collective-permute-done.8.refs_1_), channel_id=1, source_target_pairs={{2,1},{1,0},{6,5},{5,4},{10,9},{9,8},{14,13},{13,12},{18,17},{17,1... | collective-permute-start | bytes 1572872 | tf_op jit(solution)/shard_map/ppermute | solution.py:300
  108.0 15.9 %collective-permute-start.4 = (bf16[3,96,1024]{2,1,0:T(8,128)(2,1)S(1)}, bf16[3,96,1024]{2,1,0:T(8,128)(2,1)S(1)}, u32[]{:S(2)}, u32[]{:S(2)}) collective-permute-start(bf16[3,96,1024]{2,1,0:T(8,128)(2,1)S(1)} %collective-permute-done.refs_1_.refs_11_), channel_id=1, source_target_pairs={{0,4},{4,0},{8,12},{12,8},{16,20},{20,16},{24,28},{28,24},{1,5},{5... | collective-permute-start | bytes 1769480 | tf_op jit(solution)/shard_map/ppermute | solution.py:282
  109.5 14.7 %collective-permute-start.5 = (bf16[3,96,1024]{2,1,0:T(8,128)(2,1)S(1)}, bf16[3,96,1024]{2,1,0:T(8,128)(2,1)}, u32[]{:S(2)}, u32[]{:S(2)}) collective-permute-start(bf16[3,96,1024]{2,1,0:T(8,128)(2,1)S(1)} %collective-permute-done.1.refs_2_.refs_12_), channel_id=1, source_target_pairs={{0,4},{4,0},{8,12},{12,8},{16,20},{20,16},{24,28},{28,24},{1,5},{5... | collective-permute-start | bytes 1769480 | tf_op jit(solution)/shard_map/ppermute | solution.py:282
  112.8 24.5 %copy-start.20 = (bf16[2,96,1024]{2,1,0:T(8,128)(2,1)S(1)}, bf16[2,96,1024]{2,1,0:T(8,128)(2,1)}, u32[]{:S(2)}) copy-start(bf16[2,96,1024]{2,1,0:T(8,128)(2,1)} %get-tuple-element.18.refs_18_) | copy-start | bytes 1179652
  112.8 51.8 %all-to-all-start.2 = ((bf16[8,96,1024]{2,1,0:T(8,128)(2,1)}), bf16[8,96,1024]{2,1,0:T(8,128)(2,1)}, u32[]{:S(2)}, u32[]{:S(2)}) async-start(bf16[8,96,1024]{2,1,0:T(8,128)(2,1)} %get-tuple-element.17), calls=%async_computation.2 | async-start | bytes 3145728 | tf_op jit(solution)/shard_map/all_to_all | solution.py:296
  117.3 33.9 %copy-start.6 = (bf16[3,96,1024]{2,1,0:T(8,128)(2,1)}, bf16[3,96,1024]{2,1,0:T(8,128)(2,1)S(1)}, u32[]{:S(2)}) copy-start(bf16[3,96,1024]{2,1,0:T(8,128)(2,1)S(1)} %collective-permute-done.2.refs_3_.refs_13_) | copy-start | bytes 1769476
  117.3 20.2 %collective-permute-start.6 = (bf16[3,96,1024]{2,1,0:T(8,128)(2,1)S(1)}, bf16[3,96,1024]{2,1,0:T(8,128)(2,1)S(1)}, u32[]{:S(2)}, u32[]{:S(2)}) collective-permute-start(bf16[3,96,1024]{2,1,0:T(8,128)(2,1)S(1)} %collective-permute-done.2.refs_3_.refs_13_), channel_id=1, source_target_pairs={{0,4},{4,0},{8,12},{12,8},{16,20},{20,16},{24,28},{28,24},{1,5},{5... | collective-permute-start | bytes 1769480 | tf_op jit(solution)/shard_map/ppermute | solution.py:282
  117.8 6.8 %collective-permute-start.11 = (bf16[32,8192]{1,0:T(8,128)(2,1)}, bf16[32,8192]{1,0:T(8,128)(2,1)S(1)}, u32[]{:S(2)}, u32[]{:S(2)}) collective-permute-start(bf16[32,8192]{1,0:T(8,128)(2,1)} %collective-permute-done.9.refs_2_), channel_id=1, source_target_pairs={{2,3},{6,7},{10,11},{14,15},{18,19},{22,23},{26,27},{30,31}} | collective-permute-start | bytes 1572872 | tf_op jit(solution)/shard_map/ppermute | solution.py:300
  122.6 14.7 %collective-permute-start.12 = (bf16[32,8192]{1,0:T(8,128)(2,1)}, bf16[32,8192]{1,0:T(8,128)(2,1)S(1)}, u32[]{:S(2)}, u32[]{:S(2)}) collective-permute-start(bf16[32,8192]{1,0:T(8,128)(2,1)} %collective-permute-done.10.refs_3_), channel_id=1, source_target_pairs={{1,0},{5,4},{9,8},{13,12},{17,16},{21,20},{25,24},{29,28}} | collective-permute-start | bytes 1572872 | tf_op jit(solution)/shard_map/ppermute | solution.py:300
  123.9 27.3 %copy-start.7 = (bf16[3,96,1024]{2,1,0:T(8,128)(2,1)}, bf16[3,96,1024]{2,1,0:T(8,128)(2,1)S(1)}, u32[]{:S(2)}) copy-start(bf16[3,96,1024]{2,1,0:T(8,128)(2,1)S(1)} %collective-permute-done.4.refs_5_.refs_15_) | copy-start | bytes 1769476
  123.9 22.5 %collective-permute-start.39 = (bf16[2,96,1024]{2,1,0:T(8,128)(2,1)}, bf16[2,96,1024]{2,1,0:T(8,128)(2,1)}, u32[]{:S(2)}, u32[]{:S(2)}) collective-permute-start(bf16[2,96,1024]{2,1,0:T(8,128)(2,1)} %get-tuple-element.20.refs_18_), channel_id=1, source_target_pairs={{0,8},{4,20},{8,0},{12,28},{16,24},{20,4},{24,16},{28,12},{1,9},{5... | collective-permute-start | bytes 1179656 | tf_op jit(solution)/shard_map/ppermute | solution.py:282
  124.2 22.1 %collective-permute-start.40 = (bf16[2,96,1024]{2,1,0:T(8,128)(2,1)}, bf16[2,96,1024]{2,1,0:T(8,128)(2,1)}, u32[]{:S(2)}, u32[]{:S(2)}) collective-permute-start(bf16[2,96,1024]{2,1,0:T(8,128)(2,1)} %get-tuple-element.20.refs_18_), channel_id=1, source_target_pairs={{0,16},{4,12},{8,24},{12,4},{16,0},{20,28},{24,8},{28,20},{1,17},{... | collective-permute-start | bytes 1179656 | tf_op jit(solution)/shard_map/ppermute | solution.py:282
  124.6 12.8 %copy-start.13 = (bf16[32,8192]{1,0:T(8,128)(2,1)}, bf16[32,8192]{1,0:T(8,128)(2,1)S(1)}, u32[]{:S(2)}) copy-start(bf16[32,8192]{1,0:T(8,128)(2,1)S(1)} %collective-permute-done.11.refs_4_) | copy-start | bytes 1572868
  124.6 26.5 %collective-permute-start.42 = (bf16[2,96,1024]{2,1,0:T(8,128)(2,1)}, bf16[2,96,1024]{2,1,0:T(8,128)(2,1)}, u32[]{:S(2)}, u32[]{:S(2)}) collective-permute-start(bf16[2,96,1024]{2,1,0:T(8,128)(2,1)} %get-tuple-element.20.refs_18_), channel_id=1, source_target_pairs={{0,4},{4,0},{8,12},{12,8},{16,20},{20,16},{24,28},{28,24},{1,5},{5... | collective-permute-start | bytes 1179656 | tf_op jit(solution)/shard_map/ppermute | solution.py:282
  137.3 25.3 %copy-start.34 = (s32[8]{0:T(128)S(1)}, s32[8]{0:T(128)}, u32[]{:S(2)}) copy-start(s32[8]{0:T(128)} %constant.59.clone) | copy-start | bytes 100
  137.3 25.3 %copy-start.35 = (s32[8]{0:T(128)S(1)}, s32[8]{0:T(128)}, u32[]{:S(2)}) copy-start(s32[8]{0:T(128)} %constant.60.clone) | copy-start | bytes 100
  137.3 17.5 %collective-permute-start.26 = (bf16[2,96,1024]{2,1,0:T(8,128)(2,1)S(1)}, bf16[2,96,1024]{2,1,0:T(8,128)(2,1)}, u32[]{:S(2)}, u32[]{:S(2)}) collective-permute-start(bf16[2,96,1024]{2,1,0:T(8,128)(2,1)S(1)} %copy-done.20), channel_id=1, source_target_pairs={{0,8},{4,20},{8,0},{12,28},{16,24},{20,4},{24,16},{28,12},{1,9},{5... | collective-permute-start | bytes 1179656 | tf_op jit(solution)/shard_map/ppermute | solution.py:282
  137.5 13.7 %copy-start.8 = (bf16[3,96,1024]{2,1,0:T(8,128)(2,1)}, bf16[3,96,1024]{2,1,0:T(8,128)(2,1)S(1)}, u32[]{:S(2)}) copy-start(bf16[3,96,1024]{2,1,0:T(8,128)(2,1)S(1)} %collective-permute-done.6.refs_7_.refs_17_) | copy-start | bytes 1769476
  137.5 17.4 %collective-permute-start.27 = (bf16[2,96,1024]{2,1,0:T(8,128)(2,1)S(1)}, bf16[2,96,1024]{2,1,0:T(8,128)(2,1)S(1)}, u32[]{:S(2)}, u32[]{:S(2)}) collective-permute-start(bf16[2,96,1024]{2,1,0:T(8,128)(2,1)S(1)} %copy-done.20), channel_id=1, source_target_pairs={{0,16},{4,12},{8,24},{12,4},{16,0},{20,28},{24,8},{28,20},{1,17},{... | collective-permute-start | bytes 1179656 | tf_op jit(solution)/shard_map/ppermute | solution.py:282
  146.4 8.9 %collective-permute-start.29 = (bf16[2,96,1024]{2,1,0:T(8,128)(2,1)S(1)}, bf16[2,96,1024]{2,1,0:T(8,128)(2,1)S(1)}, u32[]{:S(2)}, u32[]{:S(2)}) collective-permute-start(bf16[2,96,1024]{2,1,0:T(8,128)(2,1)S(1)} %copy-done.20), channel_id=1, source_target_pairs={{0,4},{4,0},{8,12},{12,8},{16,20},{20,16},{24,28},{28,24},{1,5},{5... | collective-permute-start | bytes 1179656 | tf_op jit(solution)/shard_map/ppermute | solution.py:282
  146.4 16.2 %collective-permute-start.41 = (bf16[2,96,1024]{2,1,0:T(8,128)(2,1)}, bf16[2,96,1024]{2,1,0:T(8,128)(2,1)}, u32[]{:S(2)}, u32[]{:S(2)}) collective-permute-start(bf16[2,96,1024]{2,1,0:T(8,128)(2,1)} %collective-permute-done.39.refs_19_), channel_id=1, source_target_pairs={{0,16},{4,12},{8,24},{12,4},{16,0},{20,28},{24,8},{28,20},{1,17},{... | collective-permute-start | bytes 1179656 | tf_op jit(solution)/shard_map/ppermute | solution.py:282
  151.2 12.3 %collective-permute-start.13 = (bf16[2,96,1024]{2,1,0:T(8,128)(2,1)}, bf16[2,96,1024]{2,1,0:T(8,128)(2,1)S(1)}, u32[]{:S(2)}, u32[]{:S(2)}) collective-permute-start(bf16[2,96,1024]{2,1,0:T(8,128)(2,1)} %get-tuple-element.16.refs_18_), channel_id=1, source_target_pairs={{0,8},{4,20},{8,0},{12,28},{16,24},{20,4},{24,16},{28,12},{1,9},{5... | collective-permute-start | bytes 1179656 | tf_op jit(solution)/shard_map/ppermute | solution.py:282
  154.8 13.7 %collective-permute-start.43 = (bf16[2,96,1024]{2,1,0:T(8,128)(2,1)}, bf16[2,96,1024]{2,1,0:T(8,128)(2,1)}, u32[]{:S(2)}, u32[]{:S(2)}) collective-permute-start(bf16[2,96,1024]{2,1,0:T(8,128)(2,1)} %collective-permute-done.39.refs_19_), channel_id=1, source_target_pairs={{0,4},{4,0},{8,12},{12,8},{16,20},{20,16},{24,28},{28,24},{1,5},{5... | collective-permute-start | bytes 1179656 | tf_op jit(solution)/shard_map/ppermute | solution.py:282
  154.8 14.0 %collective-permute-start.44 = (bf16[2,96,1024]{2,1,0:T(8,128)(2,1)}, bf16[2,96,1024]{2,1,0:T(8,128)(2,1)}, u32[]{:S(2)}, u32[]{:S(2)}) collective-permute-start(bf16[2,96,1024]{2,1,0:T(8,128)(2,1)} %collective-permute-done.40.refs_20_), channel_id=1, source_target_pairs={{0,4},{4,0},{8,12},{12,8},{16,20},{20,16},{24,28},{28,24},{1,5},{5... | collective-permute-start | bytes 1179656 | tf_op jit(solution)/shard_map/ppermute | solution.py:282
  155.3 13.8 %collective-permute-start.28 = (bf16[2,96,1024]{2,1,0:T(8,128)(2,1)}, bf16[2,96,1024]{2,1,0:T(8,128)(2,1)S(1)}, u32[]{:S(2)}, u32[]{:S(2)}) collective-permute-start(bf16[2,96,1024]{2,1,0:T(8,128)(2,1)} %collective-permute-done.26.refs_19_), channel_id=1, source_target_pairs={{0,16},{4,12},{8,24},{12,4},{16,0},{20,28},{24,8},{28,20},{1,17},{... | collective-permute-start | bytes 1179656 | tf_op jit(solution)/shard_map/ppermute | solution.py:282
  162.6 8.3 %collective-permute-start.45 = (bf16[2,96,1024]{2,1,0:T(8,128)(2,1)}, bf16[2,96,1024]{2,1,0:T(8,128)(2,1)}, u32[]{:S(2)}, u32[]{:S(2)}) collective-permute-start(bf16[2,96,1024]{2,1,0:T(8,128)(2,1)} %collective-permute-done.41.refs_21_), channel_id=1, source_target_pairs={{0,4},{4,0},{8,12},{12,8},{16,20},{20,16},{24,28},{28,24},{1,5},{5... | collective-permute-start | bytes 1179656 | tf_op jit(solution)/shard_map/ppermute | solution.py:282
  163.4 23.7 %copy-start.22 = (bf16[2,96,1024]{2,1,0:T(8,128)(2,1)}, bf16[2,96,1024]{2,1,0:T(8,128)(2,1)S(1)}, u32[]{:S(2)}) copy-start(bf16[2,96,1024]{2,1,0:T(8,128)(2,1)S(1)} %collective-permute-done.13.refs_19_) | copy-start | bytes 1179652
  163.4 23.1 %collective-permute-start.14 = (bf16[2,96,1024]{2,1,0:T(8,128)(2,1)}, bf16[2,96,1024]{2,1,0:T(8,128)(2,1)}, u32[]{:S(2)}, u32[]{:S(2)}) collective-permute-start(bf16[2,96,1024]{2,1,0:T(8,128)(2,1)} %get-tuple-element.16.refs_18_), channel_id=1, source_target_pairs={{0,16},{4,12},{8,24},{12,4},{16,0},{20,28},{24,8},{28,20},{1,17},{... | collective-permute-start | bytes 1179656 | tf_op jit(solution)/shard_map/ppermute | solution.py:282
  164.6 46.6 %all-to-all-start.1 = ((bf16[8,96,1024]{2,1,0:T(8,128)(2,1)}), bf16[8,96,1024]{2,1,0:T(8,128)(2,1)S(1)}, u32[]{:S(2)}, u32[]{:S(2)}) async-start(bf16[8,96,1024]{2,1,0:T(8,128)(2,1)} %get-tuple-element.15), calls=%async_computation.1 | async-start | bytes 3145728 | tf_op jit(solution)/shard_map/all_to_all | solution.py:296
  168.5 18.0 %copy-start.21 = (bf16[2,96,1024]{2,1,0:T(8,128)(2,1)S(1)}, bf16[2,96,1024]{2,1,0:T(8,128)(2,1)}, u32[]{:S(2)}) copy-start(bf16[2,96,1024]{2,1,0:T(8,128)(2,1)} %get-tuple-element.16.refs_18_) | copy-start | bytes 1179652
  168.6 18.6 %collective-permute-start.30 = (bf16[2,96,1024]{2,1,0:T(8,128)(2,1)}, bf16[2,96,1024]{2,1,0:T(8,128)(2,1)S(1)}, u32[]{:S(2)}, u32[]{:S(2)}) collective-permute-start(bf16[2,96,1024]{2,1,0:T(8,128)(2,1)} %collective-permute-done.26.refs_19_), channel_id=1, source_target_pairs={{0,4},{4,0},{8,12},{12,8},{16,20},{20,16},{24,28},{28,24},{1,5},{5... | collective-permute-start | bytes 1179656 | tf_op jit(solution)/shard_map/ppermute | solution.py:282
  168.8 18.4 %collective-permute-start.31 = (bf16[2,96,1024]{2,1,0:T(8,128)(2,1)S(1)}, bf16[2,96,1024]{2,1,0:T(8,128)(2,1)S(1)}, u32[]{:S(2)}, u32[]{:S(2)}) collective-permute-start(bf16[2,96,1024]{2,1,0:T(8,128)(2,1)S(1)} %copy-done.24), channel_id=1, source_target_pairs={{0,4},{4,0},{8,12},{12,8},{16,20},{20,16},{24,28},{28,24},{1,5},{5... | collective-permute-start | bytes 1179656 | tf_op jit(solution)/shard_map/ppermute | solution.py:282
  169.2 17.4 %copy-start.26 = (bf16[2,96,1024]{2,1,0:T(8,128)(2,1)}, bf16[2,96,1024]{2,1,0:T(8,128)(2,1)S(1)}, u32[]{:S(2)}) copy-start(bf16[2,96,1024]{2,1,0:T(8,128)(2,1)S(1)} %collective-permute-done.28.refs_21_) | copy-start | bytes 1179652
  169.2 23.4 %collective-permute-start.15 = (bf16[2,96,1024]{2,1,0:T(8,128)(2,1)S(1)}, bf16[2,96,1024]{2,1,0:T(8,128)(2,1)S(1)}, u32[]{:S(2)}, u32[]{:S(2)}) collective-permute-start(bf16[2,96,1024]{2,1,0:T(8,128)(2,1)S(1)} %collective-permute-done.13.refs_19_), channel_id=1, source_target_pairs={{0,16},{4,12},{8,24},{12,4},{16,0},{20,28},{24,8},{28,20},{1,17},{... | collective-permute-start | bytes 1179656 | tf_op jit(solution)/shard_map/ppermute | solution.py:282
  170.9 21.8 %collective-permute-start.32 = (bf16[2,96,1024]{2,1,0:T(8,128)(2,1)S(1)}, bf16[2,96,1024]{2,1,0:T(8,128)(2,1)S(1)}, u32[]{:S(2)}, u32[]{:S(2)}) collective-permute-start(bf16[2,96,1024]{2,1,0:T(8,128)(2,1)S(1)} %collective-permute-done.28.refs_21_), channel_id=1, source_target_pairs={{0,4},{4,0},{8,12},{12,8},{16,20},{20,16},{24,28},{28,24},{1,5},{5... | collective-permute-start | bytes 1179656 | tf_op jit(solution)/shard_map/ppermute | solution.py:282
  186.6 23.7 %collective-permute-start.16 = (bf16[2,96,1024]{2,1,0:T(8,128)(2,1)S(1)}, bf16[2,96,1024]{2,1,0:T(8,128)(2,1)S(1)}, u32[]{:S(2)}, u32[]{:S(2)}) collective-permute-start(bf16[2,96,1024]{2,1,0:T(8,128)(2,1)S(1)} %copy-done.21), channel_id=1, source_target_pairs={{0,4},{4,0},{8,12},{12,8},{16,20},{20,16},{24,28},{28,24},{1,5},{5... | collective-permute-start | bytes 1179656 | tf_op jit(solution)/shard_map/ppermute | solution.py:282
  187.1 23.2 %collective-permute-start.17 = (bf16[2,96,1024]{2,1,0:T(8,128)(2,1)S(1)}, bf16[2,96,1024]{2,1,0:T(8,128)(2,1)S(1)}, u32[]{:S(2)}, u32[]{:S(2)}) collective-permute-start(bf16[2,96,1024]{2,1,0:T(8,128)(2,1)S(1)} %collective-permute-done.13.refs_19_), channel_id=1, source_target_pairs={{0,4},{4,0},{8,12},{12,8},{16,20},{20,16},{24,28},{28,24},{1,5},{5... | collective-permute-start | bytes 1179656 | tf_op jit(solution)/shard_map/ppermute | solution.py:282
  187.3 23.1 %collective-permute-start.18 = (bf16[2,96,1024]{2,1,0:T(8,128)(2,1)}, bf16[2,96,1024]{2,1,0:T(8,128)(2,1)S(1)}, u32[]{:S(2)}, u32[]{:S(2)}) collective-permute-start(bf16[2,96,1024]{2,1,0:T(8,128)(2,1)} %collective-permute-done.14.refs_20_), channel_id=1, source_target_pairs={{0,4},{4,0},{8,12},{12,8},{16,20},{20,16},{24,28},{28,24},{1,5},{5... | collective-permute-start | bytes 1179656 | tf_op jit(solution)/shard_map/ppermute | solution.py:282
  192.5 17.7 %copy-start.27 = (bf16[2,96,1024]{2,1,0:T(8,128)(2,1)}, bf16[2,96,1024]{2,1,0:T(8,128)(2,1)S(1)}, u32[]{:S(2)}) copy-start(bf16[2,96,1024]{2,1,0:T(8,128)(2,1)S(1)} %collective-permute-done.15.refs_21_) | copy-start | bytes 1179652
  192.6 18.6 %collective-permute-start.19 = (bf16[2,96,1024]{2,1,0:T(8,128)(2,1)S(1)}, bf16[2,96,1024]{2,1,0:T(8,128)(2,1)}, u32[]{:S(2)}, u32[]{:S(2)}) collective-permute-start(bf16[2,96,1024]{2,1,0:T(8,128)(2,1)S(1)} %collective-permute-done.15.refs_21_), channel_id=1, source_target_pairs={{0,4},{4,0},{8,12},{12,8},{16,20},{20,16},{24,28},{28,24},{1,5},{5... | collective-permute-start | bytes 1179656 | tf_op jit(solution)/shard_map/ppermute | solution.py:282
  (23 other events, 102.7 us)

commit v2 on v1

--- a/solution.py
+++ b/solution.py
@@ -141,7 +141,7 @@
     )(z.reshape(1), block, gram)
 
 
-def update(total, slots, components, epochs, work, steps=2):
+def update(total, slots, components, epochs, work, steps=4):
     gram = work[0][2][0][0]
     arcs = len(gram)
     height = work[0][1][0][0].shape[2]
@@ -223,7 +223,10 @@
             in_specs.extend(
                 [pl.BlockSpec((1, size, width), lambda n, m, _, block=block: (n, block, 0))] * arcs
             )
-    args = [pltpu.with_memory_space_constraint(v, pltpu.HBM) for v in args]
+    moved = {id(v) for _, rows, _ in work for v, _ in rows}
+    args = [
+        v if id(v) in moved else pltpu.with_memory_space_constraint(v, pltpu.HBM) for v in args
+    ]
     whole = pl.BlockSpec((tile, width), lambda n, m, _: (m, n))
     aliases = {}
     if not first:
@@ -315,10 +318,11 @@
 
     own = partials.reshape(components * epoch_block, param_count)
     blocks, part = place_own(z, own, gram, arc_count, share)
+    total = None
+    behind, blocks = lax.optimization_barrier((own, blocks))
     own_rows, own_columns = exchange(blocks, part)
-    total = None
     for c in range(components):
-        up = [own[c * epoch_block : (c + 1) * epoch_block]]
+        up = [(behind if c else own)[c * epoch_block : (c + 1) * epoch_block]]
         down = list(up)
         for step in range(par_count - 1):
             pairs = [(i, i + 1) for i in range(step, par_count - 1)]

time: 233 us -> 234 us (level)
  waiting for transfers between devices: 90.4 us -> 85.3 us
    ppermute x28, waiting for transfers between devices: 41.2 us -> 37.6 us  [hop(): return lax.ppermute(v, 'arc', moves)]
    ppermute x18, starting transfers between devices: 32.9 us -> 35.3 us  [along(): return lax.ppermute(v, 'par', pairs)]
    unnamed x74 -> x36, local copies, waits for them, and re-layouts: 6.24 us -> 7.22 us
  transfers between devices with their start and end apart: 50 -> 50, of which waited for: 14 -> 13; matrix products, arithmetic and copies ran while one was open for 1% -> 2% of each run, Pallas kernels for 20% -> 20%
where the time goes in v2:
time: 234 us; the launch traced here: 230 us
  waiting for transfers between devices  85.3 us (36%)
  starting transfers between devices  67.5 us (29%)
  Pallas kernels  63.8 us (27%)
  local copies, waits for them, and re-layouts  10.7 us (5%)
    pallas_call x3, Pallas kernels, update(): pl.pallas_call(body, grid_spec=pltpu.PrefetchScalarGridSpec(num_scalar_pr...  51 us
    ppermute x18, waiting for transfers between devices, along(): return lax.ppermute(v, 'par', pairs)  47.7 us
    ppermute x28, waiting for transfers between devices, hop(): return lax.ppermute(v, 'arc', moves)  37.6 us
    ppermute x18, starting transfers between devices, along(): return lax.ppermute(v, 'par', pairs)  35.3 us
    ppermute x28, starting transfers between devices, hop(): return lax.ppermute(v, 'arc', moves)  16.6 us
    all_to_all x4, starting transfers between devices, exchange(): lax.all_to_all(blocks, 'arc', split_axis=0, concat_axis=0, tiled=True)  15.6 us
    pallas_call x3, Pallas kernels, place(): pl.pallas_call(body, in_specs=[pl.BlockSpec(memory_space=pltpu.SMEM)] + [...  9.89 us
    unnamed x36, local copies, waits for them, and re-layouts  7.22 us
  transfers between devices with their start and end apart: 50, of which 13 were waited for; matrix products, arithmetic and copies ran while one was open for 2% of the time, Pallas kernels for 20%

profile of v2, /device:TPU:0, one launch (start us, length us, event | category | flops | bytes accessed | tf_op | source)
XLA Modules:
  0.0 230.5 jit_solution(5138958740521569921)
XLA Ops:
  0.0 1.9 slice_bitcast_fusion
  1.9 5.8 %collective-permute-start.33 = (bf16[32,8192]{1,0:T(8,128)(2,1)}, bf16[32,8192]{1,0:T(8,128)(2,1)}, u32[]{:S(2)}, u32[]{:S(2)}) collective-permute-start(bf16[32,8192]{1,0:T(8,128)(2,1)} %slice_bitcast_fusion), channel_id=1, source_target_pairs={{0,1},{1,2},{2,3},{4,5},{5,6},{6,7},{8,9},{9,10},{10,11},{12,13},{... | collective-permute-start | bytes 1572872 | tf_op jit(solution)/shard_map/ppermute | solution.py:303
  7.7 1.3 collective-permute-start.34
  9.1 0.7 multiply_bitcast_fusion
  10.5 0.6 gather_fusion
  11.2 1.2 fusion.18.gram_ref
  12.4 2.9 %place_own.1 = (bf16[8,96,1024]{2,1,0:T(8,128)(2,1)}, bf16[3,96,1024]{2,1,0:T(8,128)(2,1)}) custom-call(s32[1]{0:T(128)} %bitcast.z_ref, bf16[96,8192]{1,0:T(8,128)(2,1)} %bitcast.31, f32[3,128,128]{2,1,0:T(8,128)} %fusion.18.gram_ref), custom_call_target="tpu_custom_call" | custom-call | bytes 3145728 | tf_op jit(solution)/shard_map/place_own/pallas_call | solution.py:129
  15.2 3.9 %all-to-all-start = ((bf16[8,96,1024]{2,1,0:T(8,128)(2,1)}), bf16[8,96,1024]{2,1,0:T(8,128)(2,1)S(1)}, u32[]{:S(2)}, u32[]{:S(2)}) async-start(bf16[8,96,1024]{2,1,0:T(8,128)(2,1)} %get-tuple-element.17), calls=%async_computation | async-start | bytes 3145728 | tf_op jit(solution)/shard_map/all_to_all | solution.py:299
  19.1 0.7 collective-permute-start.35
  19.8 3.5 %collective-permute-done.34.refs_1_ = bf16[32,8192]{1,0:T(8,128)(2,1)} collective-permute-done((bf16[32,8192]{1,0:T(8,128)(2,1)}, bf16[32,8192]{1,0:T(8,128)(2,1)}, u32[]{:S(2)}, u32[]{:S(2)}) %collective-permute-start.34) | collective-permute-done | bytes 524320 | tf_op jit(solution)/shard_map/ppermute | solution.py:303
  23.3 1.3 collective-permute-start.36
  24.6 0.9 fusion.17
  25.5 5.3 %collective-permute-start.20 = (bf16[32,8192]{1,0:T(8,128)(2,1)S(1)}, bf16[32,8192]{1,0:T(8,128)(2,1)}, u32[]{:S(2)}, u32[]{:S(2)}) collective-permute-start(bf16[32,8192]{1,0:T(8,128)(2,1)S(1)} %get-tuple-element.25), channel_id=1, source_target_pairs={{0,1},{1,2},{2,3},{4,5},{5,6},{6,7},{8,9},{9,10},{10,11},{12,13},{... | collective-permute-start | bytes 1572872 | tf_op jit(solution)/shard_map/ppermute | solution.py:303
  30.8 1.3 collective-permute-start.21
  32.1 0.8 copy-done.4
  32.9 0.7 collective-permute-start.37
  33.6 6.6 %collective-permute-done.36.refs_3_ = bf16[32,8192]{1,0:T(8,128)(2,1)S(1)} collective-permute-done((bf16[32,8192]{1,0:T(8,128)(2,1)}, bf16[32,8192]{1,0:T(8,128)(2,1)S(1)}, u32[]{:S(2)}, u32[]{:S(2)}) %collective-permute-start.36) | collective-permute-done | bytes 524320 | tf_op jit(solution)/shard_map/ppermute | solution.py:303
  40.2 1.3 collective-permute-start.38
  41.5 5.4 %collective-permute-start.7 = (bf16[32,8192]{1,0:T(8,128)(2,1)}, bf16[32,8192]{1,0:T(8,128)(2,1)}, u32[]{:S(2)}, u32[]{:S(2)}) collective-permute-start(bf16[32,8192]{1,0:T(8,128)(2,1)} %get-tuple-element.26), channel_id=1, source_target_pairs={{0,1},{1,2},{2,3},{4,5},{5,6},{6,7},{8,9},{9,10},{10,11},{12,13},{... | collective-permute-start | bytes 1572872 | tf_op jit(solution)/shard_map/ppermute | solution.py:303
  46.9 1.3 collective-permute-start.8
  48.2 3.4 %collective-permute-done.21.refs_1_ = bf16[32,8192]{1,0:T(8,128)(2,1)} collective-permute-done((bf16[32,8192]{1,0:T(8,128)(2,1)S(1)}, bf16[32,8192]{1,0:T(8,128)(2,1)}, u32[]{:S(2)}, u32[]{:S(2)}) %collective-permute-start.21) | collective-permute-done | bytes 524320 | tf_op jit(solution)/shard_map/ppermute | solution.py:303
  51.5 1.4 collective-permute-start.22
  53.0 1.3 collective-permute-start.23
  54.3 8.4 %collective-permute-done.38.refs_5_ = bf16[32,8192]{1,0:T(8,128)(2,1)S(1)} collective-permute-done((bf16[32,8192]{1,0:T(8,128)(2,1)S(1)}, bf16[32,8192]{1,0:T(8,128)(2,1)S(1)}, u32[]{:S(2)}, u32[]{:S(2)}) %collective-permute-start.38) | collective-permute-done | bytes 524320 | tf_op jit(solution)/shard_map/ppermute | solution.py:303
  62.7 0.8 copy-done.7
  63.5 3.3 %place.5 = (bf16[8,96,1024]{2,1,0:T(8,128)(2,1)}, bf16[2,96,1024]{2,1,0:T(8,128)(2,1)}) custom-call(s32[1]{0:T(128)} %bitcast.z_ref, bf16[32,8192]{1,0:T(8,128)(2,1)} %collective-permute-done.33.refs_0_, bf16[32,8192]{1,0:T(8,128)(2,1)} %collective-permute-done.34.refs_1_, bf16[32,8192]{1,0:T(8,128)(2,1)} %copy-done.4, bf16[32,8192]{1,0:T(8,128)(2,1)} %copy-done.5, ...), custom_call_target="tpu_custom_call" | custom-call | bytes 3145728 | tf_op jit(solution)/shard_map/place/pallas_call | solution.py:92
  66.8 3.7 %all-to-all-start.3 = ((bf16[8,96,1024]{2,1,0:T(8,128)(2,1)}), bf16[8,96,1024]{2,1,0:T(8,128)(2,1)S(1)}, u32[]{:S(2)}, u32[]{:S(2)}) async-start(bf16[8,96,1024]{2,1,0:T(8,128)(2,1)} %get-tuple-element.23), calls=%async_computation.3 | async-start | bytes 3145728 | tf_op jit(solution)/shard_map/all_to_all | solution.py:299
  70.5 2.0 collective-permute-start
  72.5 1.5 collective-permute-start.1
  74.0 1.5 collective-permute-start.24
  75.5 8.4 %collective-permute-done.23.refs_3_ = bf16[32,8192]{1,0:T(8,128)(2,1)} collective-permute-done((bf16[32,8192]{1,0:T(8,128)(2,1)}, bf16[32,8192]{1,0:T(8,128)(2,1)}, u32[]{:S(2)}, u32[]{:S(2)}) %collective-permute-start.23) | collective-permute-done | bytes 524320 | tf_op jit(solution)/shard_map/ppermute | solution.py:303
  83.9 1.3 collective-permute-start.25
  85.2 18.2 %collective-permute-done.refs_1_.refs_11_ = bf16[3,96,1024]{2,1,0:T(8,128)(2,1)} collective-permute-done((bf16[3,96,1024]{2,1,0:T(8,128)(2,1)}, bf16[3,96,1024]{2,1,0:T(8,128)(2,1)}, u32[]{:S(2)}, u32[]{:S(2)}) %collective-permute-start) | collective-permute-done | bytes 589856 | tf_op jit(solution)/shard_map/ppermute | solution.py:285
  103.4 1.5 collective-permute-start.2
  104.9 1.5 collective-permute-start.9
  106.3 1.3 collective-permute-start.10
  108.2 3.3 %place.4 = (bf16[8,96,1024]{2,1,0:T(8,128)(2,1)}, bf16[2,96,1024]{2,1,0:T(8,128)(2,1)}) custom-call(s32[1]{0:T(128)} %bitcast.z_ref, bf16[32,8192]{1,0:T(8,128)(2,1)} %collective-permute-done.20.refs_0_, bf16[32,8192]{1,0:T(8,128)(2,1)} %collective-permute-done.21.refs_1_, bf16[32,8192]{1,0:T(8,128)(2,1)} %collective-permute-done.22.refs_2_, ...), custom_call_target="tpu_custom_call" | custom-call | bytes 3145728 | tf_op jit(solution)/shard_map/place/pallas_call | solution.py:92
  111.5 1.2 copy-done.1
  112.7 3.6 %all-to-all-start.2 = ((bf16[8,96,1024]{2,1,0:T(8,128)(2,1)}), bf16[8,96,1024]{2,1,0:T(8,128)(2,1)S(1)}, u32[]{:S(2)}, u32[]{:S(2)}) async-start(bf16[8,96,1024]{2,1,0:T(8,128)(2,1)} %get-tuple-element.21), calls=%async_computation.2 | async-start | bytes 3145728 | tf_op jit(solution)/shard_map/all_to_all | solution.py:299
  116.7 1.4 collective-permute-start.11
  118.1 4.8 %collective-permute-done.10.refs_3_ = bf16[32,8192]{1,0:T(8,128)(2,1)} collective-permute-done((bf16[32,8192]{1,0:T(8,128)(2,1)}, bf16[32,8192]{1,0:T(8,128)(2,1)}, u32[]{:S(2)}, u32[]{:S(2)}) %collective-permute-start.10) | collective-permute-done | bytes 524320 | tf_op jit(solution)/shard_map/ppermute | solution.py:303
  122.9 1.3 collective-permute-start.12
  125.1 12.7 %collective-permute-done.12.refs_5_ = bf16[32,8192]{1,0:T(8,128)(2,1)} collective-permute-done((bf16[32,8192]{1,0:T(8,128)(2,1)}, bf16[32,8192]{1,0:T(8,128)(2,1)}, u32[]{:S(2)}, u32[]{:S(2)}) %collective-permute-start.12) | collective-permute-done | bytes 524320 | tf_op jit(solution)/shard_map/ppermute | solution.py:303
  137.7 1.0 collective-permute-start.27
  138.8 6.6 %collective-permute-done.39.refs_19_ = bf16[2,96,1024]{2,1,0:T(8,128)(2,1)} collective-permute-done((bf16[2,96,1024]{2,1,0:T(8,128)(2,1)}, bf16[2,96,1024]{2,1,0:T(8,128)(2,1)}, u32[]{:S(2)}, u32[]{:S(2)}) %collective-permute-start.39) | collective-permute-done | bytes 393248 | tf_op jit(solution)/shard_map/ppermute | solution.py:285
  145.4 1.5 collective-permute-start.41
  146.9 3.3 %place.3 = (bf16[8,96,1024]{2,1,0:T(8,128)(2,1)}, bf16[2,96,1024]{2,1,0:T(8,128)(2,1)}) custom-call(s32[1]{0:T(128)} %bitcast.z_ref, bf16[32,8192]{1,0:T(8,128)(2,1)} %collective-permute-done.7.refs_0_, bf16[32,8192]{1,0:T(8,128)(2,1)} %collective-permute-done.8.refs_1_, bf16[32,8192]{1,0:T(8,128)(2,1)} %collective-permute-done.9.refs_2_, ...), custom_call_target="tpu_custom_call" | custom-call | bytes 3145728 | tf_op jit(solution)/shard_map/place/pallas_call | solution.py:92
  150.7 3.1 %collective-permute-done.26.refs_19_ = bf16[2,96,1024]{2,1,0:T(8,128)(2,1)} collective-permute-done((bf16[2,96,1024]{2,1,0:T(8,128)(2,1)}, bf16[2,96,1024]{2,1,0:T(8,128)(2,1)}, u32[]{:S(2)}, u32[]{:S(2)}) %collective-permute-start.26) | collective-permute-done | bytes 393248 | tf_op jit(solution)/shard_map/ppermute | solution.py:285
  154.3 1.5 collective-permute-start.28
  155.8 5.8 %collective-permute-done.41.refs_21_ = bf16[2,96,1024]{2,1,0:T(8,128)(2,1)} collective-permute-done((bf16[2,96,1024]{2,1,0:T(8,128)(2,1)}, bf16[2,96,1024]{2,1,0:T(8,128)(2,1)}, u32[]{:S(2)}, u32[]{:S(2)}) %collective-permute-start.41) | collective-permute-done | bytes 393248 | tf_op jit(solution)/shard_map/ppermute | solution.py:285
  161.6 0.9 collective-permute-done.13.refs_19_
  162.5 1.2 collective-permute-start.14
  163.7 4.5 %all-to-all-start.1 = ((bf16[8,96,1024]{2,1,0:T(8,128)(2,1)}), bf16[8,96,1024]{2,1,0:T(8,128)(2,1)}, u32[]{:S(2)}, u32[]{:S(2)}) async-start(bf16[8,96,1024]{2,1,0:T(8,128)(2,1)} %get-tuple-element.19), calls=%async_computation.1 | async-start | bytes 3145728 | tf_op jit(solution)/shard_map/all_to_all | solution.py:299
  168.8 1.7 collective-permute-start.15
  170.5 1.4 copy-done.2
  171.9 16.2 %update.3.refs_26_ = f32[1024,2048]{1,0:T(8,128)} custom-call(s32[8]{0:T(128)S(1)} %fusion.13.slot_ref, bf16[3,96,1024]{2,1,0:T(8,128)(2,1)} %get-tuple-element.15.refs_0_.refs_10_, bf16[3,96,1024]{2,1,0:T(8,128)(2,1)} %collective-permute-done.refs_1_.refs_11_, bf16[3,96,1024]{2,1,0:T(8,128)(2,1)} %collective-permute-done.1.refs_2_.refs_12_, ...), custom_call_target="tpu_custom_call" | custom-call | flops 8589934592 | bytes 16777216 | tf_op jit(solution)/shard_map/update/pallas_call | solution.py:236
  188.1 0.6 collective-permute-start.16
  189.2 3.0 %collective-permute-done.15.refs_21_ = bf16[2,96,1024]{2,1,0:T(8,128)(2,1)S(1)} collective-permute-done((bf16[2,96,1024]{2,1,0:T(8,128)(2,1)}, bf16[2,96,1024]{2,1,0:T(8,128)(2,1)S(1)}, u32[]{:S(2)}, u32[]{:S(2)}) %collective-permute-start.15) | collective-permute-done | bytes 393248 | tf_op jit(solution)/shard_map/ppermute | solution.py:285
  192.3 0.7 copy-done.15
  193.1 17.1 %update.4.refs_26_ = f32[1024,2048]{1,0:T(8,128)} custom-call(s32[8]{0:T(128)S(1)} %fusion.13.slot_ref, bf16[3,96,1024]{2,1,0:T(8,128)(2,1)} %get-tuple-element.15.refs_0_.refs_10_, bf16[3,96,1024]{2,1,0:T(8,128)(2,1)} %collective-permute-done.refs_1_.refs_11_, ...), custom_call_target="tpu_custom_call", output_to_operand_aliasing={{}: (27, {})} | custom-call | flops 8589934592 | bytes 16777216 | tf_op jit(solution)/shard_map/update/pallas_call | solution.py:236
  210.3 0.7 copy-done.11
  211.0 0.8 copy-done.13
  211.8 0.8 copy-done.14
  212.6 17.8 %update.5 = f32[1024,2048]{1,0:T(8,128)} custom-call(s32[8]{0:T(128)S(1)} %fusion.13.slot_ref, bf16[3,96,1024]{2,1,0:T(8,128)(2,1)} %get-tuple-element.15.refs_0_.refs_10_, bf16[3,96,1024]{2,1,0:T(8,128)(2,1)} %collective-permute-done.refs_1_.refs_11_, bf16[3,96,1024]{2,1,0:T(8,128)(2,1)} %collective-permute-done.1.refs_2_.refs_12_, ...), custom_call_target="tpu_custom_call", output_to_operand_aliasing={{}: (27, {})} | custom-call | flops 8589934592 | bytes 16777216 | tf_op jit(solution)/shard_map/update/pallas_call | solution.py:236
  (93 shorter events, 5.1 us)
Async XLA Ops:
  0.0 9.8 %copy-start = (f32[1,3,128,128]{3,2,1,0:T(8,128)S(1)}, f32[1,3,128,128]{3,2,1,0:T(8,128)}, u32[]{:S(2)}) copy-start(f32[1,3,128,128]{3,2,1,0:T(8,128)} %param.7) | copy-start | bytes 589828
  1.9 17.2 %collective-permute-start.33 = (bf16[32,8192]{1,0:T(8,128)(2,1)}, bf16[32,8192]{1,0:T(8,128)(2,1)}, u32[]{:S(2)}, u32[]{:S(2)}) collective-permute-start(bf16[32,8192]{1,0:T(8,128)(2,1)} %slice_bitcast_fusion), channel_id=1, source_target_pairs={{0,1},{1,2},{2,3},{4,5},{5,6},{6,7},{8,9},{9,10},{10,11},{12,13},{... | collective-permute-start | bytes 1572872 | tf_op jit(solution)/shard_map/ppermute | solution.py:303
  7.7 15.6 %collective-permute-start.34 = (bf16[32,8192]{1,0:T(8,128)(2,1)}, bf16[32,8192]{1,0:T(8,128)(2,1)}, u32[]{:S(2)}, u32[]{:S(2)}) collective-permute-start(bf16[32,8192]{1,0:T(8,128)(2,1)} %slice_bitcast_fusion), channel_id=1, source_target_pairs={{3,2},{2,1},{1,0},{7,6},{6,5},{5,4},{11,10},{10,9},{9,8},{15,14},{... | collective-permute-start | bytes 1572872 | tf_op jit(solution)/shard_map/ppermute | solution.py:303
  15.2 9.4 %copy-start.3 = (bf16[1,3,32,8192]{3,2,1,0:T(8,128)(2,1)S(1)}, bf16[1,3,32,8192]{3,2,1,0:T(8,128)(2,1)}, u32[]{:S(2)}) copy-start(bf16[1,3,32,8192]{3,2,1,0:T(8,128)(2,1)} %param.5) | copy-start | bytes 4718596
  15.2 51.5 %all-to-all-start = ((bf16[8,96,1024]{2,1,0:T(8,128)(2,1)}), bf16[8,96,1024]{2,1,0:T(8,128)(2,1)S(1)}, u32[]{:S(2)}, u32[]{:S(2)}) async-start(bf16[8,96,1024]{2,1,0:T(8,128)(2,1)} %get-tuple-element.17), calls=%async_computation | async-start | bytes 3145728 | tf_op jit(solution)/shard_map/all_to_all | solution.py:299
  19.1 13.0 %collective-permute-start.35 = (bf16[32,8192]{1,0:T(8,128)(2,1)}, bf16[32,8192]{1,0:T(8,128)(2,1)S(1)}, u32[]{:S(2)}, u32[]{:S(2)}) collective-permute-start(bf16[32,8192]{1,0:T(8,128)(2,1)} %collective-permute-done.33.refs_0_), channel_id=1, source_target_pairs={{1,2},{2,3},{5,6},{6,7},{9,10},{10,11},{13,14},{14,15},{17,18},{18... | collective-permute-start | bytes 1572872 | tf_op jit(solution)/shard_map/ppermute | solution.py:303
  23.3 16.9 %collective-permute-start.36 = (bf16[32,8192]{1,0:T(8,128)(2,1)}, bf16[32,8192]{1,0:T(8,128)(2,1)S(1)}, u32[]{:S(2)}, u32[]{:S(2)}) collective-permute-start(bf16[32,8192]{1,0:T(8,128)(2,1)} %collective-permute-done.34.refs_1_), channel_id=1, source_target_pairs={{2,1},{1,0},{6,5},{5,4},{10,9},{9,8},{14,13},{13,12},{18,17},{17,1... | collective-permute-start | bytes 1572872 | tf_op jit(solution)/shard_map/ppermute | solution.py:303
  25.5 21.4 %collective-permute-start.20 = (bf16[32,8192]{1,0:T(8,128)(2,1)S(1)}, bf16[32,8192]{1,0:T(8,128)(2,1)}, u32[]{:S(2)}, u32[]{:S(2)}) collective-permute-start(bf16[32,8192]{1,0:T(8,128)(2,1)S(1)} %get-tuple-element.25), channel_id=1, source_target_pairs={{0,1},{1,2},{2,3},{4,5},{5,6},{6,7},{8,9},{9,10},{10,11},{12,13},{... | collective-permute-start | bytes 1572872 | tf_op jit(solution)/shard_map/ppermute | solution.py:303
  30.8 20.7 %collective-permute-start.21 = (bf16[32,8192]{1,0:T(8,128)(2,1)S(1)}, bf16[32,8192]{1,0:T(8,128)(2,1)}, u32[]{:S(2)}, u32[]{:S(2)}) collective-permute-start(bf16[32,8192]{1,0:T(8,128)(2,1)S(1)} %get-tuple-element.25), channel_id=1, source_target_pairs={{3,2},{2,1},{1,0},{7,6},{6,5},{5,4},{11,10},{10,9},{9,8},{15,14},{... | collective-permute-start | bytes 1572872 | tf_op jit(solution)/shard_map/ppermute | solution.py:303
  32.1 0.8 copy-start.4
  32.9 20.1 %collective-permute-start.37 = (bf16[32,8192]{1,0:T(8,128)(2,1)S(1)}, bf16[32,8192]{1,0:T(8,128)(2,1)S(1)}, u32[]{:S(2)}, u32[]{:S(2)}) collective-permute-start(bf16[32,8192]{1,0:T(8,128)(2,1)S(1)} %collective-permute-done.35.refs_2_), channel_id=1, source_target_pairs={{2,3},{6,7},{10,11},{14,15},{18,19},{22,23},{26,27},{30,31}} | collective-permute-start | bytes 1572872 | tf_op jit(solution)/shard_map/ppermute | solution.py:303
  40.2 12.8 %copy-start.5 = (bf16[32,8192]{1,0:T(8,128)(2,1)}, bf16[32,8192]{1,0:T(8,128)(2,1)S(1)}, u32[]{:S(2)}) copy-start(bf16[32,8192]{1,0:T(8,128)(2,1)S(1)} %collective-permute-done.36.refs_3_) | copy-start | bytes 1572868
  40.2 22.5 %collective-permute-start.38 = (bf16[32,8192]{1,0:T(8,128)(2,1)S(1)}, bf16[32,8192]{1,0:T(8,128)(2,1)S(1)}, u32[]{:S(2)}, u32[]{:S(2)}) collective-permute-start(bf16[32,8192]{1,0:T(8,128)(2,1)S(1)} %collective-permute-done.36.refs_3_), channel_id=1, source_target_pairs={{1,0},{5,4},{9,8},{13,12},{17,16},{21,20},{25,24},{29,28}} | collective-permute-start | bytes 1572872 | tf_op jit(solution)/shard_map/ppermute | solution.py:303
  41.5 31.0 %collective-permute-start.7 = (bf16[32,8192]{1,0:T(8,128)(2,1)}, bf16[32,8192]{1,0:T(8,128)(2,1)}, u32[]{:S(2)}, u32[]{:S(2)}) collective-permute-start(bf16[32,8192]{1,0:T(8,128)(2,1)} %get-tuple-element.26), channel_id=1, source_target_pairs={{0,1},{1,2},{2,3},{4,5},{5,6},{6,7},{8,9},{9,10},{10,11},{12,13},{... | collective-permute-start | bytes 1572872 | tf_op jit(solution)/shard_map/ppermute | solution.py:303
  46.9 27.1 %collective-permute-start.8 = (bf16[32,8192]{1,0:T(8,128)(2,1)}, bf16[32,8192]{1,0:T(8,128)(2,1)}, u32[]{:S(2)}, u32[]{:S(2)}) collective-permute-start(bf16[32,8192]{1,0:T(8,128)(2,1)} %get-tuple-element.26), channel_id=1, source_target_pairs={{3,2},{2,1},{1,0},{7,6},{6,5},{5,4},{11,10},{10,9},{9,8},{15,14},{... | collective-permute-start | bytes 1572872 | tf_op jit(solution)/shard_map/ppermute | solution.py:303
  51.5 22.5 %collective-permute-start.22 = (bf16[32,8192]{1,0:T(8,128)(2,1)}, bf16[32,8192]{1,0:T(8,128)(2,1)}, u32[]{:S(2)}, u32[]{:S(2)}) collective-permute-start(bf16[32,8192]{1,0:T(8,128)(2,1)} %collective-permute-done.20.refs_0_), channel_id=1, source_target_pairs={{1,2},{2,3},{5,6},{6,7},{9,10},{10,11},{13,14},{14,15},{17,18},{18... | collective-permute-start | bytes 1572872 | tf_op jit(solution)/shard_map/ppermute | solution.py:303
  53.0 9.7 %copy-start.6 = (bf16[32,8192]{1,0:T(8,128)(2,1)}, bf16[32,8192]{1,0:T(8,128)(2,1)S(1)}, u32[]{:S(2)}) copy-start(bf16[32,8192]{1,0:T(8,128)(2,1)S(1)} %collective-permute-done.37.refs_4_) | copy-start | bytes 1572868
  53.0 30.9 %collective-permute-start.23 = (bf16[32,8192]{1,0:T(8,128)(2,1)}, bf16[32,8192]{1,0:T(8,128)(2,1)}, u32[]{:S(2)}, u32[]{:S(2)}) collective-permute-start(bf16[32,8192]{1,0:T(8,128)(2,1)} %collective-permute-done.21.refs_1_), channel_id=1, source_target_pairs={{2,1},{1,0},{6,5},{5,4},{10,9},{9,8},{14,13},{13,12},{18,17},{17,1... | collective-permute-start | bytes 1572872 | tf_op jit(solution)/shard_map/ppermute | solution.py:303
  62.7 0.8 copy-start.7
  66.8 44.7 %all-to-all-start.3 = ((bf16[8,96,1024]{2,1,0:T(8,128)(2,1)}), bf16[8,96,1024]{2,1,0:T(8,128)(2,1)S(1)}, u32[]{:S(2)}, u32[]{:S(2)}) async-start(bf16[8,96,1024]{2,1,0:T(8,128)(2,1)} %get-tuple-element.23), calls=%async_computation.3 | async-start | bytes 3145728 | tf_op jit(solution)/shard_map/all_to_all | solution.py:299
  70.5 32.9 %collective-permute-start = (bf16[3,96,1024]{2,1,0:T(8,128)(2,1)}, bf16[3,96,1024]{2,1,0:T(8,128)(2,1)}, u32[]{:S(2)}, u32[]{:S(2)}) collective-permute-start(bf16[3,96,1024]{2,1,0:T(8,128)(2,1)} %get-tuple-element.15.refs_0_.refs_10_), channel_id=1, source_target_pairs={{0,8},{4,20},{8,0},{12,28},{16,24},{20,4},{24,16},{28,12},{1,9},{5... | collective-permute-start | bytes 1769480 | tf_op jit(solution)/shard_map/ppermute | solution.py:285
  72.5 32.3 %collective-permute-start.1 = (bf16[3,96,1024]{2,1,0:T(8,128)(2,1)}, bf16[3,96,1024]{2,1,0:T(8,128)(2,1)}, u32[]{:S(2)}, u32[]{:S(2)}) collective-permute-start(bf16[3,96,1024]{2,1,0:T(8,128)(2,1)} %get-tuple-element.15.refs_0_.refs_10_), channel_id=1, source_target_pairs={{0,16},{4,12},{8,24},{12,4},{16,0},{20,28},{24,8},{28,20},{1,17},{... | collective-permute-start | bytes 1769480 | tf_op jit(solution)/shard_map/ppermute | solution.py:285
  74.0 32.3 %collective-permute-start.3 = (bf16[3,96,1024]{2,1,0:T(8,128)(2,1)}, bf16[3,96,1024]{2,1,0:T(8,128)(2,1)}, u32[]{:S(2)}, u32[]{:S(2)}) collective-permute-start(bf16[3,96,1024]{2,1,0:T(8,128)(2,1)} %get-tuple-element.15.refs_0_.refs_10_), channel_id=1, source_target_pairs={{0,4},{4,0},{8,12},{12,8},{16,20},{20,16},{24,28},{28,24},{1,5},{5... | collective-permute-start | bytes 1769480 | tf_op jit(solution)/shard_map/ppermute | solution.py:285
  74.0 33.6 %collective-permute-start.24 = (bf16[32,8192]{1,0:T(8,128)(2,1)}, bf16[32,8192]{1,0:T(8,128)(2,1)}, u32[]{:S(2)}, u32[]{:S(2)}) collective-permute-start(bf16[32,8192]{1,0:T(8,128)(2,1)} %collective-permute-done.22.refs_2_), channel_id=1, source_target_pairs={{2,3},{6,7},{10,11},{14,15},{18,19},{22,23},{26,27},{30,31}} | collective-permute-start | bytes 1572872 | tf_op jit(solution)/shard_map/ppermute | solution.py:303
  83.9 23.8 %collective-permute-start.25 = (bf16[32,8192]{1,0:T(8,128)(2,1)}, bf16[32,8192]{1,0:T(8,128)(2,1)}, u32[]{:S(2)}, u32[]{:S(2)}) collective-permute-start(bf16[32,8192]{1,0:T(8,128)(2,1)} %collective-permute-done.23.refs_3_), channel_id=1, source_target_pairs={{1,0},{5,4},{9,8},{13,12},{17,16},{21,20},{25,24},{29,28}} | collective-permute-start | bytes 1572872 | tf_op jit(solution)/shard_map/ppermute | solution.py:303
  103.4 12.9 %collective-permute-start.2 = (bf16[3,96,1024]{2,1,0:T(8,128)(2,1)}, bf16[3,96,1024]{2,1,0:T(8,128)(2,1)}, u32[]{:S(2)}, u32[]{:S(2)}) collective-permute-start(bf16[3,96,1024]{2,1,0:T(8,128)(2,1)} %collective-permute-done.refs_1_.refs_11_), channel_id=1, source_target_pairs={{0,16},{4,12},{8,24},{12,4},{16,0},{20,28},{24,8},{28,20},{1,17},{... | collective-permute-start | bytes 1769480 | tf_op jit(solution)/shard_map/ppermute | solution.py:285
  104.9 11.8 %collective-permute-start.9 = (bf16[32,8192]{1,0:T(8,128)(2,1)}, bf16[32,8192]{1,0:T(8,128)(2,1)}, u32[]{:S(2)}, u32[]{:S(2)}) collective-permute-start(bf16[32,8192]{1,0:T(8,128)(2,1)} %collective-permute-done.7.refs_0_), channel_id=1, source_target_pairs={{1,2},{2,3},{5,6},{6,7},{9,10},{10,11},{13,14},{14,15},{17,18},{18... | collective-permute-start | bytes 1572872 | tf_op jit(solution)/shard_map/ppermute | solution.py:303
  106.3 16.5 %collective-permute-start.10 = (bf16[32,8192]{1,0:T(8,128)(2,1)}, bf16[32,8192]{1,0:T(8,128)(2,1)}, u32[]{:S(2)}, u32[]{:S(2)}) collective-permute-start(bf16[32,8192]{1,0:T(8,128)(2,1)} %collective-permute-done.8.refs_1_), channel_id=1, source_target_pairs={{2,1},{1,0},{6,5},{5,4},{10,9},{9,8},{14,13},{13,12},{18,17},{17,1... | collective-permute-start | bytes 1572872 | tf_op jit(solution)/shard_map/ppermute | solution.py:303
  107.6 16.5 %collective-permute-start.4 = (bf16[3,96,1024]{2,1,0:T(8,128)(2,1)}, bf16[3,96,1024]{2,1,0:T(8,128)(2,1)}, u32[]{:S(2)}, u32[]{:S(2)}) collective-permute-start(bf16[3,96,1024]{2,1,0:T(8,128)(2,1)} %collective-permute-done.refs_1_.refs_11_), channel_id=1, source_target_pairs={{0,4},{4,0},{8,12},{12,8},{16,20},{20,16},{24,28},{28,24},{1,5},{5... | collective-permute-start | bytes 1769480 | tf_op jit(solution)/shard_map/ppermute | solution.py:285
  107.7 16.8 %collective-permute-start.5 = (bf16[3,96,1024]{2,1,0:T(8,128)(2,1)}, bf16[3,96,1024]{2,1,0:T(8,128)(2,1)}, u32[]{:S(2)}, u32[]{:S(2)}) collective-permute-start(bf16[3,96,1024]{2,1,0:T(8,128)(2,1)} %collective-permute-done.1.refs_2_.refs_12_), channel_id=1, source_target_pairs={{0,4},{4,0},{8,12},{12,8},{16,20},{20,16},{24,28},{28,24},{1,5},{5... | collective-permute-start | bytes 1769480 | tf_op jit(solution)/shard_map/ppermute | solution.py:285
  111.5 1.2 copy-start.1
  112.7 51.1 %all-to-all-start.2 = ((bf16[8,96,1024]{2,1,0:T(8,128)(2,1)}), bf16[8,96,1024]{2,1,0:T(8,128)(2,1)S(1)}, u32[]{:S(2)}, u32[]{:S(2)}) async-start(bf16[8,96,1024]{2,1,0:T(8,128)(2,1)} %get-tuple-element.21), calls=%async_computation.2 | async-start | bytes 3145728 | tf_op jit(solution)/shard_map/all_to_all | solution.py:299
  116.3 21.5 %collective-permute-start.6 = (bf16[3,96,1024]{2,1,0:T(8,128)(2,1)}, bf16[3,96,1024]{2,1,0:T(8,128)(2,1)}, u32[]{:S(2)}, u32[]{:S(2)}) collective-permute-start(bf16[3,96,1024]{2,1,0:T(8,128)(2,1)} %collective-permute-done.2.refs_3_.refs_13_), channel_id=1, source_target_pairs={{0,4},{4,0},{8,12},{12,8},{16,20},{20,16},{24,28},{28,24},{1,5},{5... | collective-permute-start | bytes 1769480 | tf_op jit(solution)/shard_map/ppermute | solution.py:285
  116.7 8.4 %collective-permute-start.11 = (bf16[32,8192]{1,0:T(8,128)(2,1)}, bf16[32,8192]{1,0:T(8,128)(2,1)}, u32[]{:S(2)}, u32[]{:S(2)}) collective-permute-start(bf16[32,8192]{1,0:T(8,128)(2,1)} %collective-permute-done.9.refs_2_), channel_id=1, source_target_pairs={{2,3},{6,7},{10,11},{14,15},{18,19},{22,23},{26,27},{30,31}} | collective-permute-start | bytes 1572872 | tf_op jit(solution)/shard_map/ppermute | solution.py:303
  122.9 14.9 %collective-permute-start.12 = (bf16[32,8192]{1,0:T(8,128)(2,1)}, bf16[32,8192]{1,0:T(8,128)(2,1)}, u32[]{:S(2)}, u32[]{:S(2)}) collective-permute-start(bf16[32,8192]{1,0:T(8,128)(2,1)} %collective-permute-done.10.refs_3_), channel_id=1, source_target_pairs={{1,0},{5,4},{9,8},{13,12},{17,16},{21,20},{25,24},{29,28}} | collective-permute-start | bytes 1572872 | tf_op jit(solution)/shard_map/ppermute | solution.py:303
  124.2 21.2 %collective-permute-start.39 = (bf16[2,96,1024]{2,1,0:T(8,128)(2,1)}, bf16[2,96,1024]{2,1,0:T(8,128)(2,1)}, u32[]{:S(2)}, u32[]{:S(2)}) collective-permute-start(bf16[2,96,1024]{2,1,0:T(8,128)(2,1)} %get-tuple-element.24.refs_18_), channel_id=1, source_target_pairs={{0,8},{4,20},{8,0},{12,28},{16,24},{20,4},{24,16},{28,12},{1,9},{5... | collective-permute-start | bytes 1179656 | tf_op jit(solution)/shard_map/ppermute | solution.py:285
  124.5 20.9 %collective-permute-start.40 = (bf16[2,96,1024]{2,1,0:T(8,128)(2,1)}, bf16[2,96,1024]{2,1,0:T(8,128)(2,1)}, u32[]{:S(2)}, u32[]{:S(2)}) collective-permute-start(bf16[2,96,1024]{2,1,0:T(8,128)(2,1)} %get-tuple-element.24.refs_18_), channel_id=1, source_target_pairs={{0,16},{4,12},{8,24},{12,4},{16,0},{20,28},{24,8},{28,20},{1,17},{... | collective-permute-start | bytes 1179656 | tf_op jit(solution)/shard_map/ppermute | solution.py:285
  125.1 25.1 %collective-permute-start.42 = (bf16[2,96,1024]{2,1,0:T(8,128)(2,1)}, bf16[2,96,1024]{2,1,0:T(8,128)(2,1)}, u32[]{:S(2)}, u32[]{:S(2)}) collective-permute-start(bf16[2,96,1024]{2,1,0:T(8,128)(2,1)} %get-tuple-element.24.refs_18_), channel_id=1, source_target_pairs={{0,4},{4,0},{8,12},{12,8},{16,20},{20,16},{24,28},{28,24},{1,5},{5... | collective-permute-start | bytes 1179656 | tf_op jit(solution)/shard_map/ppermute | solution.py:285
  137.7 23.9 %copy-start.16 = (s32[8]{0:T(128)S(1)}, s32[8]{0:T(128)}, u32[]{:S(2)}) copy-start(s32[8]{0:T(128)} %constant.59.clone) | copy-start | bytes 100
  137.7 23.9 %copy-start.17 = (s32[8]{0:T(128)S(1)}, s32[8]{0:T(128)}, u32[]{:S(2)}) copy-start(s32[8]{0:T(128)} %constant.60.clone) | copy-start | bytes 100
  137.7 16.1 %collective-permute-start.26 = (bf16[2,96,1024]{2,1,0:T(8,128)(2,1)}, bf16[2,96,1024]{2,1,0:T(8,128)(2,1)}, u32[]{:S(2)}, u32[]{:S(2)}) collective-permute-start(bf16[2,96,1024]{2,1,0:T(8,128)(2,1)} %get-tuple-element.22.refs_18_), channel_id=1, source_target_pairs={{0,8},{4,20},{8,0},{12,28},{16,24},{20,4},{24,16},{28,12},{1,9},{5... | collective-permute-start | bytes 1179656 | tf_op jit(solution)/shard_map/ppermute | solution.py:285
  137.7 16.1 %collective-permute-start.27 = (bf16[2,96,1024]{2,1,0:T(8,128)(2,1)}, bf16[2,96,1024]{2,1,0:T(8,128)(2,1)}, u32[]{:S(2)}, u32[]{:S(2)}) collective-permute-start(bf16[2,96,1024]{2,1,0:T(8,128)(2,1)} %get-tuple-element.22.refs_18_), channel_id=1, source_target_pairs={{0,16},{4,12},{8,24},{12,4},{16,0},{20,28},{24,8},{28,20},{1,17},{... | collective-permute-start | bytes 1179656 | tf_op jit(solution)/shard_map/ppermute | solution.py:285
  145.4 8.9 %collective-permute-start.29 = (bf16[2,96,1024]{2,1,0:T(8,128)(2,1)}, bf16[2,96,1024]{2,1,0:T(8,128)(2,1)}, u32[]{:S(2)}, u32[]{:S(2)}) collective-permute-start(bf16[2,96,1024]{2,1,0:T(8,128)(2,1)} %get-tuple-element.22.refs_18_), channel_id=1, source_target_pairs={{0,4},{4,0},{8,12},{12,8},{16,20},{20,16},{24,28},{28,24},{1,5},{5... | collective-permute-start | bytes 1179656 | tf_op jit(solution)/shard_map/ppermute | solution.py:285
  145.4 16.2 %collective-permute-start.41 = (bf16[2,96,1024]{2,1,0:T(8,128)(2,1)}, bf16[2,96,1024]{2,1,0:T(8,128)(2,1)}, u32[]{:S(2)}, u32[]{:S(2)}) collective-permute-start(bf16[2,96,1024]{2,1,0:T(8,128)(2,1)} %collective-permute-done.39.refs_19_), channel_id=1, source_target_pairs={{0,16},{4,12},{8,24},{12,4},{16,0},{20,28},{24,8},{28,20},{1,17},{... | collective-permute-start | bytes 1179656 | tf_op jit(solution)/shard_map/ppermute | solution.py:285
  150.2 12.3 %collective-permute-start.13 = (bf16[2,96,1024]{2,1,0:T(8,128)(2,1)}, bf16[2,96,1024]{2,1,0:T(8,128)(2,1)}, u32[]{:S(2)}, u32[]{:S(2)}) collective-permute-start(bf16[2,96,1024]{2,1,0:T(8,128)(2,1)} %get-tuple-element.20.refs_18_), channel_id=1, source_target_pairs={{0,8},{4,20},{8,0},{12,28},{16,24},{20,4},{24,16},{28,12},{1,9},{5... | collective-permute-start | bytes 1179656 | tf_op jit(solution)/shard_map/ppermute | solution.py:285
  153.8 14.4 %collective-permute-start.43 = (bf16[2,96,1024]{2,1,0:T(8,128)(2,1)}, bf16[2,96,1024]{2,1,0:T(8,128)(2,1)}, u32[]{:S(2)}, u32[]{:S(2)}) collective-permute-start(bf16[2,96,1024]{2,1,0:T(8,128)(2,1)} %collective-permute-done.39.refs_19_), channel_id=1, source_target_pairs={{0,4},{4,0},{8,12},{12,8},{16,20},{20,16},{24,28},{28,24},{1,5},{5... | collective-permute-start | bytes 1179656 | tf_op jit(solution)/shard_map/ppermute | solution.py:285
  153.8 14.6 %collective-permute-start.44 = (bf16[2,96,1024]{2,1,0:T(8,128)(2,1)}, bf16[2,96,1024]{2,1,0:T(8,128)(2,1)}, u32[]{:S(2)}, u32[]{:S(2)}) collective-permute-start(bf16[2,96,1024]{2,1,0:T(8,128)(2,1)} %collective-permute-done.40.refs_20_), channel_id=1, source_target_pairs={{0,4},{4,0},{8,12},{12,8},{16,20},{20,16},{24,28},{28,24},{1,5},{5... | collective-permute-start | bytes 1179656 | tf_op jit(solution)/shard_map/ppermute | solution.py:285
  154.3 14.5 %collective-permute-start.28 = (bf16[2,96,1024]{2,1,0:T(8,128)(2,1)}, bf16[2,96,1024]{2,1,0:T(8,128)(2,1)}, u32[]{:S(2)}, u32[]{:S(2)}) collective-permute-start(bf16[2,96,1024]{2,1,0:T(8,128)(2,1)} %collective-permute-done.26.refs_19_), channel_id=1, source_target_pairs={{0,16},{4,12},{8,24},{12,4},{16,0},{20,28},{24,8},{28,20},{1,17},{... | collective-permute-start | bytes 1179656 | tf_op jit(solution)/shard_map/ppermute | solution.py:285
  161.6 8.9 %collective-permute-start.45 = (bf16[2,96,1024]{2,1,0:T(8,128)(2,1)}, bf16[2,96,1024]{2,1,0:T(8,128)(2,1)}, u32[]{:S(2)}, u32[]{:S(2)}) collective-permute-start(bf16[2,96,1024]{2,1,0:T(8,128)(2,1)} %collective-permute-done.41.refs_21_), channel_id=1, source_target_pairs={{0,4},{4,0},{8,12},{12,8},{16,20},{20,16},{24,28},{28,24},{1,5},{5... | collective-permute-start | bytes 1179656 | tf_op jit(solution)/shard_map/ppermute | solution.py:285
  162.5 25.6 %collective-permute-start.14 = (bf16[2,96,1024]{2,1,0:T(8,128)(2,1)}, bf16[2,96,1024]{2,1,0:T(8,128)(2,1)}, u32[]{:S(2)}, u32[]{:S(2)}) collective-permute-start(bf16[2,96,1024]{2,1,0:T(8,128)(2,1)} %get-tuple-element.20.refs_18_), channel_id=1, source_target_pairs={{0,16},{4,12},{8,24},{12,4},{16,0},{20,28},{24,8},{28,20},{1,17},{... | collective-permute-start | bytes 1179656 | tf_op jit(solution)/shard_map/ppermute | solution.py:285
  163.7 48.8 %all-to-all-start.1 = ((bf16[8,96,1024]{2,1,0:T(8,128)(2,1)}), bf16[8,96,1024]{2,1,0:T(8,128)(2,1)}, u32[]{:S(2)}, u32[]{:S(2)}) async-start(bf16[8,96,1024]{2,1,0:T(8,128)(2,1)} %get-tuple-element.19), calls=%async_computation.1 | async-start | bytes 3145728 | tf_op jit(solution)/shard_map/all_to_all | solution.py:299
  168.2 20.4 %collective-permute-start.30 = (bf16[2,96,1024]{2,1,0:T(8,128)(2,1)}, bf16[2,96,1024]{2,1,0:T(8,128)(2,1)S(1)}, u32[]{:S(2)}, u32[]{:S(2)}) collective-permute-start(bf16[2,96,1024]{2,1,0:T(8,128)(2,1)} %collective-permute-done.26.refs_19_), channel_id=1, source_target_pairs={{0,4},{4,0},{8,12},{12,8},{16,20},{20,16},{24,28},{28,24},{1,5},{5... | collective-permute-start | bytes 1179656 | tf_op jit(solution)/shard_map/ppermute | solution.py:285
  168.4 20.3 %collective-permute-start.31 = (bf16[2,96,1024]{2,1,0:T(8,128)(2,1)}, bf16[2,96,1024]{2,1,0:T(8,128)(2,1)S(1)}, u32[]{:S(2)}, u32[]{:S(2)}) collective-permute-start(bf16[2,96,1024]{2,1,0:T(8,128)(2,1)} %collective-permute-done.27.refs_20_), channel_id=1, source_target_pairs={{0,4},{4,0},{8,12},{12,8},{16,20},{20,16},{24,28},{28,24},{1,5},{5... | collective-permute-start | bytes 1179656 | tf_op jit(solution)/shard_map/ppermute | solution.py:285
  168.8 23.4 %collective-permute-start.15 = (bf16[2,96,1024]{2,1,0:T(8,128)(2,1)}, bf16[2,96,1024]{2,1,0:T(8,128)(2,1)S(1)}, u32[]{:S(2)}, u32[]{:S(2)}) collective-permute-start(bf16[2,96,1024]{2,1,0:T(8,128)(2,1)} %collective-permute-done.13.refs_19_), channel_id=1, source_target_pairs={{0,16},{4,12},{8,24},{12,4},{16,0},{20,28},{24,8},{28,20},{1,17},{... | collective-permute-start | bytes 1179656 | tf_op jit(solution)/shard_map/ppermute | solution.py:285
  170.5 21.8 %collective-permute-start.32 = (bf16[2,96,1024]{2,1,0:T(8,128)(2,1)}, bf16[2,96,1024]{2,1,0:T(8,128)(2,1)S(1)}, u32[]{:S(2)}, u32[]{:S(2)}) collective-permute-start(bf16[2,96,1024]{2,1,0:T(8,128)(2,1)} %collective-permute-done.28.refs_21_), channel_id=1, source_target_pairs={{0,4},{4,0},{8,12},{12,8},{16,20},{20,16},{24,28},{28,24},{1,5},{5... | collective-permute-start | bytes 1179656 | tf_op jit(solution)/shard_map/ppermute | solution.py:285
  170.5 1.4 copy-start.2
  171.9 16.2 %copy-start.8 = (bf16[2,96,1024]{2,1,0:T(8,128)(2,1)S(1)}, bf16[2,96,1024]{2,1,0:T(8,128)(2,1)}, u32[]{:S(2)}) copy-start(bf16[2,96,1024]{2,1,0:T(8,128)(2,1)} %get-tuple-element.20.refs_18_) | copy-start | bytes 1179652
  188.1 22.1 %collective-permute-start.16 = (bf16[2,96,1024]{2,1,0:T(8,128)(2,1)S(1)}, bf16[2,96,1024]{2,1,0:T(8,128)(2,1)S(1)}, u32[]{:S(2)}, u32[]{:S(2)}) collective-permute-start(bf16[2,96,1024]{2,1,0:T(8,128)(2,1)S(1)} %copy-done.8), channel_id=1, source_target_pairs={{0,4},{4,0},{8,12},{12,8},{16,20},{20,16},{24,28},{28,24},{1,5},{5... | collective-permute-start | bytes 1179656 | tf_op jit(solution)/shard_map/ppermute | solution.py:285
  188.7 3.7 %copy-start.10 = (bf16[2,96,1024]{2,1,0:T(8,128)(2,1)}, bf16[2,96,1024]{2,1,0:T(8,128)(2,1)S(1)}, u32[]{:S(2)}) copy-start(bf16[2,96,1024]{2,1,0:T(8,128)(2,1)S(1)} %collective-permute-done.30.refs_23_) | copy-start | bytes 1179652
  188.7 22.3 %collective-permute-start.17 = (bf16[2,96,1024]{2,1,0:T(8,128)(2,1)}, bf16[2,96,1024]{2,1,0:T(8,128)(2,1)S(1)}, u32[]{:S(2)}, u32[]{:S(2)}) collective-permute-start(bf16[2,96,1024]{2,1,0:T(8,128)(2,1)} %collective-permute-done.13.refs_19_), channel_id=1, source_target_pairs={{0,4},{4,0},{8,12},{12,8},{16,20},{20,16},{24,28},{28,24},{1,5},{5... | collective-permute-start | bytes 1179656 | tf_op jit(solution)/shard_map/ppermute | solution.py:285
  188.8 3.6 %copy-start.12 = (bf16[2,96,1024]{2,1,0:T(8,128)(2,1)}, bf16[2,96,1024]{2,1,0:T(8,128)(2,1)S(1)}, u32[]{:S(2)}) copy-start(bf16[2,96,1024]{2,1,0:T(8,128)(2,1)S(1)} %collective-permute-done.31.refs_24_) | copy-start | bytes 1179652
  188.8 23.0 %collective-permute-start.18 = (bf16[2,96,1024]{2,1,0:T(8,128)(2,1)}, bf16[2,96,1024]{2,1,0:T(8,128)(2,1)S(1)}, u32[]{:S(2)}, u32[]{:S(2)}) collective-permute-start(bf16[2,96,1024]{2,1,0:T(8,128)(2,1)} %collective-permute-done.14.refs_20_), channel_id=1, source_target_pairs={{0,4},{4,0},{8,12},{12,8},{16,20},{20,16},{24,28},{28,24},{1,5},{5... | collective-permute-start | bytes 1179656 | tf_op jit(solution)/shard_map/ppermute | solution.py:285
  192.2 18.0 %copy-start.9 = (bf16[2,96,1024]{2,1,0:T(8,128)(2,1)}, bf16[2,96,1024]{2,1,0:T(8,128)(2,1)S(1)}, u32[]{:S(2)}) copy-start(bf16[2,96,1024]{2,1,0:T(8,128)(2,1)S(1)} %collective-permute-done.15.refs_21_) | copy-start | bytes 1179652
  192.2 20.3 %collective-permute-start.19 = (bf16[2,96,1024]{2,1,0:T(8,128)(2,1)S(1)}, bf16[2,96,1024]{2,1,0:T(8,128)(2,1)}, u32[]{:S(2)}, u32[]{:S(2)}) collective-permute-start(bf16[2,96,1024]{2,1,0:T(8,128)(2,1)S(1)} %collective-permute-done.15.refs_21_), channel_id=1, source_target_pairs={{0,4},{4,0},{8,12},{12,8},{16,20},{20,16},{24,28},{28,24},{1,5},{5... | collective-permute-start | bytes 1179656 | tf_op jit(solution)/shard_map/ppermute | solution.py:285
  (4 other events, 3.0 us)
